TPU v7x, 256 devices: a whole 4x4x8 slice. The times are simulated.
256 devices in a mesh: dom: 64 (over x, z_hi, y), blk: 4 (over z_lo, core).
Axes of the slice: x: 4, y: 4, z: 8 (z_hi: 4, z_lo: 2; z = z_hi * 2 + z_lo), core: 2. Of those that a mesh axis runs over, the one named last changes fastest.
Arguments:
- adjoint_start: float32 [1536, 3, 320], P('dom', None, 'blk'), may hold values from -6 to 6
- right_sides: float32 [1536, 3, 320], P('dom', None, 'blk'), may hold values from -6 to 6
- jac_blocks: bfloat16 [1536, 7, 320, 320], P('dom', None, 'blk'), may hold values from -0.125 to 0.125
- block_inverse: bfloat16 [1536, 320, 320], P('dom', 'blk'), may hold values from -0.15625 to 0.15625
- neighbours: int32 [1536, 6], P('dom'), may hold values from 0 to 1535, as said below
- pseudo_shift: float32 [1536], P('dom'), may hold values from 0.25 to 2
- shape_partials: bfloat16 [1536, 320, 192], P('dom', 'blk'), may hold values from -0.3125 to 0.3125
- node_ids: int32 [1536, 64], P('dom'), may hold values from 0 to 49151, as said below
Outputs:
- adjoint: float32 [1536, 3, 320], P('dom', None, 'blk')
- shape_gradient: float32 [9, 49152], P(None, ('dom', 'blk'))
Inputs may be any that keep to these rules, and one draw needn't show every extreme that they name: `neighbours`: partition k holds elements k * 24 to (k + 1) * 24 - 1; every neighbour of an element lies in its own partition or in the partition just before or after it. `node_ids`: partition k owns mesh nodes k * 768 to (k + 1) * 768 - 1; every node of an element is owned by the element's partition or by the partition just before or after it.
All inputs are finite; a program needn't handle non-finite values.
Results may differ from a plain program's by a relative error of at most 0.0038.
Values may be sent and summed in bfloat16 or wider, within the bound.
A program may use at most 64 MiB of HBM per device.

v0:
```python
import jax
import jax.numpy as jnp
from jax import lax
from jax.sharding import PartitionSpec as P

RHS = 3
SWEEPS = 2
NODE_DEV = 768


def padded(block, sides, width):
    for axis, dim in sides:
        count = lax.axis_size(axis)
        forward = [(i, i + 1) for i in range(count - 1)]
        backward = [(target, source) for source, target in forward]
        low = lax.ppermute(
            lax.slice_in_dim(block, block.shape[dim] - width, None, axis=dim), axis, forward
        )
        high = lax.ppermute(lax.slice_in_dim(block, 0, width, axis=dim), axis, backward)
        block = jnp.concatenate([low, block, high], axis=dim)
    return block


def passed_along(block, axis, distance):
    devices = range(lax.axis_size(axis))
    route = [(i - distance, i) for i in devices if i - distance in devices]
    return lax.ppermute(block, axis, route)


def local(
    adjoint_start,
    right_sides,
    jac_blocks,
    block_inverse,
    neighbours,
    pseudo_shift,
    shape_partials,
    node_ids,
):
    local_count = neighbours.shape[0]
    part_index = lax.axis_index("dom")
    first_slot = (part_index - 1) * local_count
    self_slots = jnp.arange(local_count, dtype=jnp.int32)[:, None] + local_count
    slots = jnp.concatenate([self_slots, neighbours - first_slot], axis=1)
    adjoint = adjoint_start
    for sweep in range(SWEEPS):
        adj_half = adjoint.astype(jnp.bfloat16)
        columns = lax.all_gather(adj_half, "blk", axis=2, tiled=True)
        extended = padded(columns, (("dom", 0),), local_count)
        picked = extended[slots]
        product = jnp.einsum(
            "ekrc,ekjc->ejr", jac_blocks, picked, preferred_element_type=jnp.float32
        )
        image = pseudo_shift[:, None, None] * adjoint + product
        resid_half = (right_sides - image).astype(jnp.bfloat16)
        resid_full = lax.all_gather(resid_half, "blk", axis=2, tiled=True)
        adjoint = adjoint + jnp.einsum(
            "erc,ejc->ejr", block_inverse, resid_full, preferred_element_type=jnp.float32
        )
    final_half = adjoint.astype(jnp.bfloat16)
    weighted = -jnp.einsum(
        "ejr,erq->ejq", final_half, shape_partials, preferred_element_type=jnp.float32
    )
    node_width = node_ids.shape[1]
    weighted = weighted.reshape(local_count, RHS, node_width, 3)
    values = jnp.transpose(weighted, (0, 2, 1, 3)).reshape(local_count * node_width, RHS * 3)
    node_slots = (node_ids - (part_index - 1) * NODE_DEV).reshape(-1)
    partial_sums = jax.ops.segment_sum(values, node_slots, 3 * NODE_DEV).T
    lower_part = partial_sums[:, :NODE_DEV]
    middle_part = partial_sums[:, NODE_DEV : 2 * NODE_DEV]
    upper_part = partial_sums[:, 2 * NODE_DEV :]
    from_above = passed_along(lower_part, "dom", -1)
    from_below = passed_along(upper_part, "dom", 1)
    owned = middle_part + from_above + from_below
    shape_gradient = lax.psum_scatter(owned, "blk", scatter_dimension=1, tiled=True)
    return (adjoint, shape_gradient)


def solution(mesh):
    in_specs = (
        P("dom", None, "blk"),
        P("dom", None, "blk"),
        P("dom", None, "blk", None),
        P("dom", "blk", None),
        P("dom", None),
        P("dom"),
        P("dom", "blk", None),
        P("dom", None),
    )
    out_specs = (P("dom", None, "blk"), P(None, ("dom", "blk")))
    return jax.shard_map(local, mesh=mesh, in_specs=in_specs, out_specs=out_specs, check_vma=False)
```

profile of v0, /device:TPU:7, one launch (start us, length us, event | category | flops | bytes accessed | tf_op | source)
XLA Modules:
  0.0 153.2 jit_solution(12407695913070051930)
XLA Ops:
  7.3 0.9 convert_element_type.15
  8.1 0.1 copy.93
  8.2 7.0 %all_gather.12 = bf16[24,3,320]{0,1,2:T(4,128)(2,1)S(1)} all-gather(bf16[24,3,80]{0,1,2:T(4,128)(2,1)S(1)} %copy.93), channel_id=1, replica_groups=mesh['dom'=64,'blk'=4] {'blk'}, dimensions={2}, use_global_device_ids=true | all-gather | bytes 57600 | tf_op jit(solution)/shard_map/all_gather | solution.py:48
  15.3 0.2 copy.94
  15.5 10.1 %collective-permute-start.1 = (bf16[24,3,320]{2,1,0:T(4,128)(2,1)S(1)}, bf16[24,3,320]{2,1,0:T(4,128)(2,1)S(1)}, u32[]{:S(2)}, u32[]{:S(2)}) collective-permute-start(bf16[24,3,320]{2,1,0:T(4,128)(2,1)S(1)} %copy.94), channel_id=1, source_target_pairs={{4,0},{8,4},{12,8},{16,12},{20,16},{24,20},{28,24},{32,28},{36,32}... | collective-permute-start | bytes 138248 | tf_op jit(solution)/shard_map/ppermute | solution.py:19
  25.6 1.9 %collective-permute-start = (bf16[24,3,320]{2,1,0:T(4,128)(2,1)S(1)}, bf16[24,3,320]{2,1,0:T(4,128)(2,1)S(1)}, u32[]{:S(2)}, u32[]{:S(2)}) collective-permute-start(bf16[24,3,320]{2,1,0:T(4,128)(2,1)S(1)} %copy.94), channel_id=1, source_target_pairs={{0,4},{4,8},{8,12},{12,16},{16,20},{20,24},{24,28},{28,32},{32,36}... | collective-permute-start | bytes 138248 | tf_op jit(solution)/shard_map/ppermute | solution.py:16
  27.6 0.7 subtract_bitcast_fusion
  28.3 0.1 copy.98
  28.4 0.1 reshape.91
  28.5 0.1 collective-permute-done.1
  28.6 8.8 %collective-permute-done = bf16[24,3,320]{2,1,0:T(4,128)(2,1)S(1)} collective-permute-done((bf16[24,3,320]{2,1,0:T(4,128)(2,1)S(1)}, bf16[24,3,320]{2,1,0:T(4,128)(2,1)S(1)}, u32[]{:S(2)}, u32[]{:S(2)}) %collective-permute-start) | collective-permute-done | bytes 46112 | tf_op jit(solution)/shard_map/ppermute | solution.py:16
  37.4 0.2 pad_maximum_fusion
  37.6 1.1 gather_fusion
  38.8 6.8 %fusion.4 = bf16[24,3,80]{2,1,0:T(4,128)(2,1)S(1)} fusion(bf16[24,7,3,320]{3,2,1,0:T(4,128)(2,1)S(1)} %bitcast.48, bf16[24,7,80,320]{3,2,1,0:T(8,128)(2,1)} %param.10, f32[24,3,80]{2,0,1:T(8,128)S(1)} %copy-done.3, f32[24,3,80]{2,0,1:T(8,128)S(1)} %copy-done.2, f32[24]{0:T(128)S(1)} %copy-done.5), kind=kOutput, calls=%fused_computation.12 | convolution fusion | flops 25827840 | bytes 8981856 | tf_op jit(solution)/shard_map/ekrc,ekjc->ejr/dot_general | solution.py:51
  45.6 0.1 copy.102
  45.8 6.9 %all_gather.13 = bf16[24,3,320]{0,1,2:T(4,128)(2,1)S(1)} all-gather(bf16[24,3,80]{0,1,2:T(4,128)(2,1)S(1)} %copy.102), channel_id=1, replica_groups=mesh['dom'=64,'blk'=4] {'blk'}, dimensions={2}, use_global_device_ids=true | all-gather | bytes 57600 | tf_op jit(solution)/shard_map/all_gather | solution.py:56
  52.7 0.2 copy.103
  52.9 0.6 fusion.11
  53.5 0.1 copy.105
  53.7 7.1 %all_gather.14 = bf16[24,3,320]{0,1,2:T(4,128)(2,1)S(1)} all-gather(bf16[24,3,80]{0,1,2:T(4,128)(2,1)S(1)} %copy.105), channel_id=1, replica_groups=mesh['dom'=64,'blk'=4] {'blk'}, dimensions={2}, use_global_device_ids=true | all-gather | bytes 57600 | tf_op jit(solution)/shard_map/all_gather | solution.py:48
  60.8 0.2 copy.106
  61.0 1.9 %collective-permute-start.3 = (bf16[24,3,320]{2,1,0:T(4,128)(2,1)S(1)}, bf16[24,3,320]{2,1,0:T(4,128)(2,1)S(1)}, u32[]{:S(2)}, u32[]{:S(2)}) collective-permute-start(bf16[24,3,320]{2,1,0:T(4,128)(2,1)S(1)} %copy.106), channel_id=1, source_target_pairs={{4,0},{8,4},{12,8},{16,12},{20,16},{24,20},{28,24},{32,28},{36,32}... | collective-permute-start | bytes 138248 | tf_op jit(solution)/shard_map/ppermute | solution.py:19
  63.0 3.4 %collective-permute-start.2 = (bf16[24,3,320]{2,1,0:T(4,128)(2,1)S(1)}, bf16[24,3,320]{2,1,0:T(4,128)(2,1)S(1)}, u32[]{:S(2)}, u32[]{:S(2)}) collective-permute-start(bf16[24,3,320]{2,1,0:T(4,128)(2,1)S(1)} %copy.106), channel_id=1, source_target_pairs={{0,4},{4,8},{8,12},{12,16},{16,20},{20,24},{24,28},{28,32},{32,36}... | collective-permute-start | bytes 138248 | tf_op jit(solution)/shard_map/ppermute | solution.py:16
  66.4 0.1 reshape.107
  66.4 0.2 collective-permute-done.3
  66.7 7.1 %collective-permute-done.2 = bf16[24,3,320]{2,1,0:T(4,128)(2,1)S(1)} collective-permute-done((bf16[24,3,320]{2,1,0:T(4,128)(2,1)S(1)}, bf16[24,3,320]{2,1,0:T(4,128)(2,1)S(1)}, u32[]{:S(2)}, u32[]{:S(2)}) %collective-permute-start.2) | collective-permute-done | bytes 46112 | tf_op jit(solution)/shard_map/ppermute | solution.py:16
  73.7 0.2 pad_maximum_fusion.1
  73.9 1.1 gather_fusion.1
  75.1 6.8 %fusion.5 = bf16[24,3,80]{2,1,0:T(4,128)(2,1)S(1)} fusion(bf16[24,7,3,320]{3,2,1,0:T(4,128)(2,1)S(1)} %bitcast.47, bf16[24,7,80,320]{3,2,1,0:T(8,128)(2,1)} %param.10, f32[24,3,80]{2,0,1:T(8,128)S(1)} %copy-done.3, f32[24,3,80]{2,1,0:T(4,128)S(1)} %get-tuple-element.17, f32[24]{0:T(128)S(1)} %copy-done.5), kind=kOutput, calls=%fused_computation.13 | convolution fusion | flops 25827840 | bytes 8981856 | tf_op jit(solution)/shard_map/ekrc,ekjc->ejr/dot_general | solution.py:51
  81.9 0.1 copy.112
  82.0 7.5 %all_gather.15 = bf16[24,3,320]{0,1,2:T(4,128)(2,1)S(1)} all-gather(bf16[24,3,80]{0,1,2:T(4,128)(2,1)S(1)} %copy.112), channel_id=1, replica_groups=mesh['dom'=64,'blk'=4] {'blk'}, dimensions={2}, use_global_device_ids=true | all-gather | bytes 57600 | tf_op jit(solution)/shard_map/all_gather | solution.py:56
  89.6 0.2 copy.113
  89.8 0.6 convolution_add_fusion
  90.4 0.3 convolution_negate_fusion
  90.7 0.2 copy.114
  90.9 0.1 reshape.87
  91.0 0.1 copy.115
  91.1 0.1 reshape.109
  91.2 0.3 copy.116
  91.5 9.0 %scatter_custom_fusion = f32[2304,9]{1,0:T(8,128)S(1)} fusion(s32[1536]{0:T(1024)S(1)} %reshape.107, f32[1536,9]{1,0:T(8,128)S(1)} %copy.116, f32[]{:T(128)} %constant.18.clone.1), kind=kCustom, calls=%fused_computation.14 | custom fusion | flops 13824 | bytes 82948 | tf_op jit(solution)/shard_map/scatter-add | solution.py:68
  100.6 1.9 %collective-permute-start.4 = (f32[9,768]{0,1:T(8,128)S(1)}, f32[9,768]{0,1:T(8,128)S(1)}, u32[]{:S(2)}, u32[]{:S(2)}) collective-permute-start(f32[9,768]{0,1:T(8,128)S(1)} %get-tuple-element.14), channel_id=1, source_target_pairs={{4,0},{8,4},{12,8},{16,12},{20,16},{24,20},{28,24},{32,28},{36,32}... | collective-permute-start | bytes 82952 | tf_op jit(solution)/shard_map/ppermute | solution.py:27
  102.5 3.4 %collective-permute-start.5 = (f32[9,768]{0,1:T(8,128)S(1)}, f32[9,768]{0,1:T(8,128)S(1)}, u32[]{:S(2)}, u32[]{:S(2)}) collective-permute-start(f32[9,768]{0,1:T(8,128)S(1)} %get-tuple-element.15), channel_id=1, source_target_pairs={{0,4},{4,8},{8,12},{12,16},{16,20},{20,24},{24,28},{28,32},{32,36}... | collective-permute-start | bytes 82952 | tf_op jit(solution)/shard_map/ppermute | solution.py:27
  105.9 13.5 %collective-permute-done.4 = f32[9,768]{0,1:T(8,128)S(1)} collective-permute-done((f32[9,768]{0,1:T(8,128)S(1)}, f32[9,768]{0,1:T(8,128)S(1)}, u32[]{:S(2)}, u32[]{:S(2)}) %collective-permute-start.4) | collective-permute-done | bytes 27680 | tf_op jit(solution)/shard_map/ppermute | solution.py:27
  119.4 8.8 %collective-permute-done.5 = f32[9,768]{0,1:T(8,128)S(1)} collective-permute-done((f32[9,768]{0,1:T(8,128)S(1)}, f32[9,768]{0,1:T(8,128)S(1)}, u32[]{:S(2)}, u32[]{:S(2)}) %collective-permute-start.5) | collective-permute-done | bytes 27680 | tf_op jit(solution)/shard_map/ppermute | solution.py:27
  128.2 0.8 fusion.8
  129.1 0.6 copy.117
  129.7 15.1 %reduce-scatter.2.cloned.1.call-done = f32[9,192]{0,1:T(8,128)} async-done(((f32[9,768]{0,1:T(8,128)}), f32[9,192]{0,1:T(8,128)}) %reduce-scatter.2.cloned.1.call-update) | async-done | bytes 6928 | tf_op jit(solution)/shard_map/reduce_scatter | solution.py:75
  144.8 1.6 %copy.118 = f32[9,192]{1,0:T(8,128)} copy(f32[9,192]{0,1:T(8,128)} %reduce-scatter.2.cloned.1.call-done) | data formatting | bytes 13824
  (19 shorter events, 0.2 us)
Async XLA Ops:
  7.2 45.8 %copy-start = (bf16[24,80,320]{2,1,0:T(8,128)(2,1)S(1)}, bf16[24,80,320]{2,1,0:T(8,128)(2,1)}, u32[]{:S(2)}) copy-start(bf16[24,80,320]{2,1,0:T(8,128)(2,1)} %param.11) | copy-start | bytes 3686404
  7.2 31.6 %copy-start.2 = (f32[24,3,80]{2,0,1:T(8,128)S(1)}, f32[24,3,80]{2,0,1:T(8,128)}, u32[]{:S(2)}) copy-start(f32[24,3,80]{2,0,1:T(8,128)} %param.8) | copy-start | bytes 69124
  7.2 31.6 %copy-start.5 = (f32[24]{0:T(128)S(1)}, f32[24]{0:T(128)}, u32[]{:S(2)}) copy-start(f32[24]{0:T(128)} %param.13) | copy-start | bytes 292
  7.2 31.6 %copy-start.3 = (f32[24,3,80]{2,0,1:T(8,128)S(1)}, f32[24,3,80]{2,0,1:T(8,128)}, u32[]{:S(2)}) copy-start(f32[24,3,80]{2,0,1:T(8,128)} %param.9) | copy-start | bytes 69124
  7.2 137.5 %reduce-scatter.2.cloned.1.call-start = ((), (), s32[]{:S(2)}) async-start(), calls=%async_computation.1 | async-start | bytes 491520 | tf_op jit(solution)/shard_map/reduce_scatter | solution.py:75
  15.5 13.1 %collective-permute-start.1 = (bf16[24,3,320]{2,1,0:T(4,128)(2,1)S(1)}, bf16[24,3,320]{2,1,0:T(4,128)(2,1)S(1)}, u32[]{:S(2)}, u32[]{:S(2)}) collective-permute-start(bf16[24,3,320]{2,1,0:T(4,128)(2,1)S(1)} %copy.94), channel_id=1, source_target_pairs={{4,0},{8,4},{12,8},{16,12},{20,16},{24,20},{28,24},{32,28},{36,32}... | collective-permute-start | bytes 138248 | tf_op jit(solution)/shard_map/ppermute | solution.py:19
  25.6 11.8 %collective-permute-start = (bf16[24,3,320]{2,1,0:T(4,128)(2,1)S(1)}, bf16[24,3,320]{2,1,0:T(4,128)(2,1)S(1)}, u32[]{:S(2)}, u32[]{:S(2)}) collective-permute-start(bf16[24,3,320]{2,1,0:T(4,128)(2,1)S(1)} %copy.94), channel_id=1, source_target_pairs={{0,4},{4,8},{8,12},{12,16},{16,20},{20,24},{24,28},{28,32},{32,36}... | collective-permute-start | bytes 138248 | tf_op jit(solution)/shard_map/ppermute | solution.py:16
  52.7 13.6 %copy-start.4 = (s32[24,64]{1,0:T(8,128)S(1)}, s32[24,64]{1,0:T(8,128)}, u32[]{:S(2)}) copy-start(s32[24,64]{1,0:T(8,128)} %param.15) | copy-start | bytes 18436
  61.0 5.6 %collective-permute-start.3 = (bf16[24,3,320]{2,1,0:T(4,128)(2,1)S(1)}, bf16[24,3,320]{2,1,0:T(4,128)(2,1)S(1)}, u32[]{:S(2)}, u32[]{:S(2)}) collective-permute-start(bf16[24,3,320]{2,1,0:T(4,128)(2,1)S(1)} %copy.106), channel_id=1, source_target_pairs={{4,0},{8,4},{12,8},{16,12},{20,16},{24,20},{28,24},{32,28},{36,32}... | collective-permute-start | bytes 138248 | tf_op jit(solution)/shard_map/ppermute | solution.py:19
  63.0 10.8 %collective-permute-start.2 = (bf16[24,3,320]{2,1,0:T(4,128)(2,1)S(1)}, bf16[24,3,320]{2,1,0:T(4,128)(2,1)S(1)}, u32[]{:S(2)}, u32[]{:S(2)}) collective-permute-start(bf16[24,3,320]{2,1,0:T(4,128)(2,1)S(1)} %copy.106), channel_id=1, source_target_pairs={{0,4},{4,8},{8,12},{12,16},{16,20},{20,24},{24,28},{28,32},{32,36}... | collective-permute-start | bytes 138248 | tf_op jit(solution)/shard_map/ppermute | solution.py:16
  81.9 8.5 %copy-start.1 = (bf16[24,80,192]{2,1,0:T(8,128)(2,1)S(1)}, bf16[24,80,192]{2,1,0:T(8,128)(2,1)}, u32[]{:S(2)}) copy-start(bf16[24,80,192]{2,1,0:T(8,128)(2,1)} %param.14) | copy-start | bytes 2211844
  100.6 18.8 %collective-permute-start.4 = (f32[9,768]{0,1:T(8,128)S(1)}, f32[9,768]{0,1:T(8,128)S(1)}, u32[]{:S(2)}, u32[]{:S(2)}) collective-permute-start(f32[9,768]{0,1:T(8,128)S(1)} %get-tuple-element.14), channel_id=1, source_target_pairs={{4,0},{8,4},{12,8},{16,12},{20,16},{24,20},{28,24},{32,28},{36,32}... | collective-permute-start | bytes 82952 | tf_op jit(solution)/shard_map/ppermute | solution.py:27
  102.5 25.7 %collective-permute-start.5 = (f32[9,768]{0,1:T(8,128)S(1)}, f32[9,768]{0,1:T(8,128)S(1)}, u32[]{:S(2)}, u32[]{:S(2)}) collective-permute-start(f32[9,768]{0,1:T(8,128)S(1)} %get-tuple-element.15), channel_id=1, source_target_pairs={{0,4},{4,8},{8,12},{12,16},{16,20},{20,24},{24,28},{28,32},{32,36}... | collective-permute-start | bytes 82952 | tf_op jit(solution)/shard_map/ppermute | solution.py:27
Sparse Core Ops, SparseCore 0:
  129.2 15.5 reduce-scatter.1
where the time goes:
time: 155 us; the launch traced here: 153 us
  waiting for transfers between devices  53.7 us (35%)
  blocking collectives  28.6 us (18%)
  starting transfers between devices  22.6 us (15%)
  matrix products  15.2 us (10%)
  between operations  14.3 us (9%)
  other arithmetic  11.8 us (8%)
  local copies, waits for them, and re-layouts  7.05 us (5%)
    ppermute x2, waiting for transfers between devices, passed_along(): return lax.ppermute(block, axis, route)  22.3 us
    ppermute x2, waiting for transfers between devices, padded(): lax.ppermute(lax.slice_in_dim(block, block.shape[dim] - width, None, axis...  15.9 us
    reduce_scatter x1, waiting for transfers between devices, local(): lax.psum_scatter(owned, 'blk', scatter_dimension=1, tiled=True)  15.1 us
    all_gather x2, blocking collectives, local(): resid_full = lax.all_gather(resid_half, 'blk', axis=2, tiled=True)  14.5 us
    all_gather x2, blocking collectives, local(): columns = lax.all_gather(adj_half, 'blk', axis=2, tiled=True)  14.2 us
    dot_general x2, matrix products, local(): jnp.einsum('ekrc,ekjc->ejr', jac_blocks, picked, preferred_element_type=j...  13.7 us
    ppermute x2, starting transfers between devices, padded(): lax.ppermute(lax.slice_in_dim(block, 0, width, axis=dim), axis, backward)  12 us
    scatter-add x1, other arithmetic, local(): partial_sums = jax.ops.segment_sum(values, node_slots, 3 * NODE_DEV).T  9.03 us
  transfers between devices with their start and end apart: 7, of which 7 were waited for; matrix products, arithmetic and copies ran while one was open for 1% of the time, Pallas kernels for 0%

commit v1 on v0

v1 whole, which is shorter than its diff:
```python
import functools

import jax
import jax.numpy as jnp
from jax import lax
from jax.experimental import pallas as pl
from jax.experimental.pallas import tpu as pltpu
from jax.sharding import PartitionSpec as P

RHS = 3
SWEEPS = 2
NODE_DEV = 768
MESH = pl.DeviceIdType.MESH


def _halo_partners(nb):
    return [(delta, m) for delta in (-1, 0, 1) for m in range(nb) if (delta, m) != (0, 0)]


def _barrier(partners, in_range, d, b, nb):
    barrier = pltpu.get_barrier_semaphore()
    for delta, m in partners:
        @pl.when(in_range(d + delta))
        def _(delta=delta, m=m):
            pl.semaphore_signal(
                barrier, 1, device_id=(d + delta, (b + m) % nb), device_id_type=MESH
            )
    nd = lax.axis_size("dom")
    has_lower = (d + nd - 1) // nd
    has_upper = (2 * nd - 2 - d) // nd
    peers = [sum(1 for delta, _ in partners if delta == side) for side in (-1, 0, 1)]
    pl.semaphore_wait(barrier, peers[1] + peers[0] * has_lower + peers[2] * has_upper)


def _halo_gather_kernel(x_ref, out_ref, buf, send_sem, recv_sem):
    d, b = lax.axis_index("dom"), lax.axis_index("blk")
    nd, nb = lax.axis_size("dom"), lax.axis_size("blk")
    partners = _halo_partners(nb)

    def in_range(i):
        return (i >= 0) & (i < nd)

    _barrier(partners, in_range, d, b, nb)

    def outgoing(delta, m):
        return pltpu.make_async_remote_copy(
            src_ref=x_ref,
            dst_ref=buf.at[1 - delta, b],
            send_sem=send_sem.at[delta + 1, m],
            recv_sem=recv_sem.at[1 - delta, b],
            device_id=(d + delta, (b + m) % nb),
            device_id_type=MESH,
        )

    for delta, m in partners:
        pl.when(in_range(d + delta))(lambda delta=delta, m=m: outgoing(delta, m).start())
    buf[1, b] = x_ref[...]
    for side in (-1, 1):
        @pl.when(jnp.logical_not(in_range(d + side)))
        def _(side=side):
            buf[1 + side] = jnp.zeros(buf.shape[1:], buf.dtype)
    for delta, m in partners:
        pl.when(in_range(d + delta))(lambda delta=delta, m=m: outgoing(delta, m).wait_send())
    for delta, m in partners:
        p, s = 1 + delta, (b + m) % nb

        @pl.when(in_range(d + delta))
        def _(p=p, s=s):
            pltpu.make_async_remote_copy(
                src_ref=x_ref,
                dst_ref=buf.at[p, s],
                send_sem=send_sem.at[p, 0],
                recv_sem=recv_sem.at[p, s],
                device_id=(d + p - 1, s),
                device_id_type=MESH,
            ).wait_recv()

    out_ref[...] = buf[...]


def _blk_gather_kernel(x_ref, out_ref, buf, send_sem, recv_sem):
    d, b = lax.axis_index("dom"), lax.axis_index("blk")
    nd, nb = lax.axis_size("dom"), lax.axis_size("blk")
    partners = [(0, m) for m in range(1, nb)]
    _barrier(partners, lambda i: (i >= 0) & (i < nd), d, b, nb)

    def outgoing(m):
        return pltpu.make_async_remote_copy(
            src_ref=x_ref,
            dst_ref=buf.at[b],
            send_sem=send_sem.at[m],
            recv_sem=recv_sem.at[b],
            device_id=(d, (b + m) % nb),
            device_id_type=MESH,
        )

    for _, m in partners:
        outgoing(m).start()
    buf[b] = x_ref[...]
    for _, m in partners:
        outgoing(m).wait_send()
    for _, m in partners:
        s = (b + m) % nb
        pltpu.make_async_remote_copy(
            src_ref=x_ref,
            dst_ref=buf.at[s],
            send_sem=send_sem.at[0],
            recv_sem=recv_sem.at[s],
            device_id=(d, s),
            device_id_type=MESH,
        ).wait_recv()
    out_ref[...] = buf[...]


def _node_reduce_kernel(x_ref, out_ref, buf, send_sem, recv_sem):
    d, b = lax.axis_index("dom"), lax.axis_index("blk")
    nd, nb = lax.axis_size("dom"), lax.axis_size("blk")
    partners = _halo_partners(nb)

    def in_range(i):
        return (i >= 0) & (i < nd)

    _barrier(partners, in_range, d, b, nb)

    def outgoing(delta, m):
        p = 1 + delta
        return pltpu.make_async_remote_copy(
            src_ref=x_ref.at[p, (b + m) % nb],
            dst_ref=buf.at[p, b],
            send_sem=send_sem.at[p, m],
            recv_sem=recv_sem.at[p, b],
            device_id=(d + delta, (b + m) % nb),
            device_id_type=MESH,
        )

    for delta, m in partners:
        pl.when(in_range(d + delta))(lambda delta=delta, m=m: outgoing(delta, m).start())
    out_ref[...] = x_ref[1, b]
    for delta, m in partners:
        pl.when(in_range(d + delta))(lambda delta=delta, m=m: outgoing(delta, m).wait_send())
    for delta, m in partners:
        p, s = 1 + delta, (b + m) % nb

        @pl.when(in_range(d - delta))
        def _(p=p, s=s):
            pltpu.make_async_remote_copy(
                src_ref=x_ref.at[p, s],
                dst_ref=buf.at[p, s],
                send_sem=send_sem.at[p, 0],
                recv_sem=recv_sem.at[p, s],
                device_id=(d - delta, s),
                device_id_type=MESH,
            ).wait_recv()
            out_ref[...] += buf[p, s]


def _exchange(kernel, x, out_shape, buf_shape, sem_shape, collective_id):
    return pl.pallas_call(
        kernel,
        out_shape=jax.ShapeDtypeStruct(out_shape, x.dtype),
        in_specs=[pl.BlockSpec(memory_space=pltpu.VMEM)],
        out_specs=pl.BlockSpec(memory_space=pltpu.VMEM),
        scratch_shapes=[
            pltpu.VMEM(buf_shape, x.dtype),
            pltpu.SemaphoreType.DMA(sem_shape),
            pltpu.SemaphoreType.DMA(sem_shape),
        ],
        compiler_params=pltpu.CompilerParams(
            collective_id=collective_id, has_side_effects=True
        ),
    )(x)


def halo_gather(x, nb, collective_id):
    shape = (3, nb) + x.shape
    out = _exchange(_halo_gather_kernel, x, shape, shape, (3, nb), collective_id)
    e, r, c = x.shape
    return jnp.transpose(out, (0, 2, 3, 1, 4)).reshape(3 * e, r, nb * c)


def blk_gather(x, nb, collective_id):
    shape = (nb,) + x.shape
    out = _exchange(_blk_gather_kernel, x, shape, shape, (nb,), collective_id)
    e, r, c = x.shape
    return jnp.transpose(out, (1, 2, 0, 3)).reshape(e, r, nb * c)


def node_reduce(chunks, collective_id):
    nb = chunks.shape[1]
    return _exchange(
        _node_reduce_kernel, chunks, chunks.shape[2:], chunks.shape, (3, nb), collective_id
    )


def local(
    adjoint_start,
    right_sides,
    jac_blocks,
    block_inverse,
    neighbours,
    pseudo_shift,
    shape_partials,
    node_ids,
):
    local_count = neighbours.shape[0]
    nb = lax.axis_size("blk")
    part_index = lax.axis_index("dom")
    first_slot = (part_index - 1) * local_count
    self_slots = jnp.arange(local_count, dtype=jnp.int32)[:, None] + local_count
    slots = jnp.concatenate([self_slots, neighbours - first_slot], axis=1)
    adjoint = adjoint_start
    for sweep in range(SWEEPS):
        adj_half = adjoint.astype(jnp.bfloat16)
        extended = halo_gather(adj_half, nb, collective_id=2 * sweep)
        picked = extended[slots]
        product = jnp.einsum(
            "ekrc,ekjc->ejr", jac_blocks, picked, preferred_element_type=jnp.float32
        )
        image = pseudo_shift[:, None, None] * adjoint + product
        resid_half = (right_sides - image).astype(jnp.bfloat16)
        resid_full = blk_gather(resid_half, nb, collective_id=2 * sweep + 1)
        adjoint = adjoint + jnp.einsum(
            "erc,ejc->ejr", block_inverse, resid_full, preferred_element_type=jnp.float32
        )
    final_half = adjoint.astype(jnp.bfloat16)
    weighted = -jnp.einsum(
        "ejr,erq->ejq", final_half, shape_partials, preferred_element_type=jnp.float32
    )
    node_width = node_ids.shape[1]
    weighted = weighted.reshape(local_count, RHS, node_width, 3)
    values = jnp.transpose(weighted, (0, 2, 1, 3)).reshape(local_count * node_width, RHS * 3)
    node_slots = (node_ids - (part_index - 1) * NODE_DEV).reshape(-1)
    partial_sums = jax.ops.segment_sum(values, node_slots, 3 * NODE_DEV).T
    chunks = jnp.transpose(
        partial_sums.reshape(RHS * 3, 3, nb, NODE_DEV // nb), (1, 2, 0, 3)
    )
    shape_gradient = node_reduce(chunks, collective_id=2 * SWEEPS)
    return (adjoint, shape_gradient)


def solution(mesh):
    in_specs = (
        P("dom", None, "blk"),
        P("dom", None, "blk"),
        P("dom", None, "blk", None),
        P("dom", "blk", None),
        P("dom", None),
        P("dom"),
        P("dom", "blk", None),
        P("dom", None),
    )
    out_specs = (P("dom", None, "blk"), P(None, ("dom", "blk")))
    return jax.shard_map(local, mesh=mesh, in_specs=in_specs, out_specs=out_specs, check_vma=False)
```

time: 155 us -> 100 us (0.65); the launches traced: 153 us -> 99.8 us
  Pallas kernels: 0 us -> 58.5 us
  waiting for transfers between devices: 53.7 us -> 0 us
  blocking collectives: 28.6 us -> 0 us
  starting transfers between devices: 22.6 us -> 0 us
  between operations: 14.3 us -> 0.83 us
  local copies, waits for them, and re-layouts: 7.05 us -> 12.1 us
  matrix products: 15.2 us -> 17 us
    pallas_call x0 -> x5, Pallas kernels: none -> 58.5 us  [_exchange(): pl.pallas_call(kernel, out_shape=jax.ShapeDtypeStruct(out_shape, x.dtype)...]
    ppermute x6 -> x0, waiting for transfers between devices: 38.6 us -> none  [the longest x2 22.3 us: passed_along(): return lax.ppermute(block, axis, route)]
    all_gather x4 -> x0, blocking collectives: 28.6 us -> none  [the longest x2 14.5 us: local(): resid_full = lax.all_gather(resid_half, 'blk', axis=2, tiled=True)]
    ppermute x6 -> x0, starting transfers between devices: 22.6 us -> none  [the longest x2 12 us: padded(): lax.ppermute(lax.slice_in_dim(block, 0, width, axis=dim), axis, backward)]
    reduce_scatter x1 -> x0, waiting for transfers between devices: 15.1 us -> none  [local(): lax.psum_scatter(owned, 'blk', scatter_dimension=1, tiled=True)]
    reshape x0 -> x9, local copies, waits for them, and re-layouts: none -> 6.17 us  [the longest x4 2.85 us: halo_gather(): return jnp.transpose(out, (0, 2, 3, 1, 4)).reshape(3 * e, r, nb * c)]
  transfers between devices with their start and end apart: 7 -> 0, of which waited for: 7 -> 0; matrix products, arithmetic and copies ran while one was open for 1% -> 0% of each run, Pallas kernels for 0% -> 0%
where the time goes in v1:
time: 100 us; the launch traced here: 99.8 us
  Pallas kernels  58.5 us (58%)
  matrix products  17 us (17%)
  local copies, waits for them, and re-layouts  12.1 us (12%)
  other arithmetic  11.3 us (11%)
    pallas_call x5, Pallas kernels, _exchange(): pl.pallas_call(kernel, out_shape=jax.ShapeDtypeStruct(out_shape, x.dtype)...  58.5 us
    dot_general x2, matrix products, local(): jnp.einsum('ekrc,ekjc->ejr', jac_blocks, picked, preferred_element_type=j...  14.9 us
    scatter-add x1, other arithmetic, local(): partial_sums = jax.ops.segment_sum(values, node_slots, 3 * NODE_DEV).T  9.03 us
    reshape x4, local copies, waits for them, and re-layouts, halo_gather(): return jnp.transpose(out, (0, 2, 3, 1, 4)).reshape(3 * e, r, nb * c)  2.85 us
    gather x2, local copies, waits for them, and re-layouts, local(): picked = extended[slots]  2.28 us
    reshape x4, local copies, waits for them, and re-layouts, blk_gather(): return jnp.transpose(out, (1, 2, 0, 3)).reshape(e, r, nb * c)  2.18 us

profile of v1, /device:TPU:7, one launch (start us, length us, event | category | flops | bytes accessed | tf_op | source)
XLA Modules:
  0.0 99.8 jit_solution(13644792715631670293)
XLA Ops:
  0.6 0.0 copy-start
  0.6 0.0 copy-start.2
  0.7 0.0 copy-start.4
  0.7 0.0 copy-start.3
  0.7 0.8 subtract_bitcast_fusion
  1.5 0.1 copy.65
  1.6 0.1 reshape.111
  1.7 0.7 broadcast_subtract_fusion
  2.4 0.1 reshape.127
  2.5 0.8 convert_element_type.15
  3.3 0.6 copy.62.x_ref
  3.9 18.2 %shard_map.95 = bf16[3,4,24,3,80]{4,3,2,1,0:T(4,128)(2,1)} custom-call(bf16[24,3,80]{2,1,0:T(4,128)(2,1)} %copy.62.x_ref), custom_call_target="tpu_custom_call" | custom-call | tf_op jit(solution)/shard_map/pallas_call | solution.py:158
  22.1 1.1 %copy.88 = bf16[3,24,3,4,80]{4,3,2,1,0:T(4,128)(2,1)S(1)} copy(bf16[3,24,3,4,80]{4,2,1,3,0:T(4,128)(2,1)} %bitcast.56) | data formatting | bytes 276480 | tf_op jit(solution)/shard_map/reshape | solution.py:178
  23.2 0.3 reshape.138
  23.5 1.1 %gather_fusion = bf16[168,3,320]{2,1,0:T(4,128)(2,1)S(1)} fusion(bf16[72,3,320]{2,1,0:T(4,128)(2,1)S(1)} %reshape.138, s32[1024]{0:T(1024)S(1)} %pad_clamp_fusion), kind=kCustom, calls=%fused_computation | custom fusion | bytes 645792 | tf_op jit(solution)/shard_map/gather | solution.py:215
  24.6 0.0 copy-done.2
  24.7 0.0 copy-done.4
  24.7 0.0 copy-done.3
  24.7 7.5 %fusion.4.x_ref = bf16[24,3,80]{2,1,0:T(4,128)(2,1)} fusion(bf16[24,7,3,320]{3,2,1,0:T(4,128)(2,1)S(1)} %bitcast.54, bf16[24,7,80,320]{3,2,1,0:T(8,128)(2,1)} %param.10, f32[24,3,80]{2,0,1:T(8,128)S(1)} %copy-done.3, f32[24,3,80]{2,0,1:T(8,128)S(1)} %copy-done.2, f32[24]{0:T(128)S(1)} %copy-done.4), kind=kOutput, calls=%fused_computation.12 | convolution fusion | flops 25827840 | bytes 8981856 | tf_op jit(solution)/shard_map/ekrc,ekjc->ejr/dot_general | solution.py:216
  32.1 5.8 %shard_map.96 = bf16[4,24,3,80]{3,2,1,0:T(4,128)(2,1)} custom-call(bf16[24,3,80]{2,1,0:T(4,128)(2,1)} %fusion.4.x_ref), custom_call_target="tpu_custom_call" | custom-call | tf_op jit(solution)/shard_map/pallas_call | solution.py:158
  37.9 0.9 copy.90
  38.8 0.1 reshape.139
  39.0 0.0 copy-done
  39.0 1.2 %fusion.9 = (bf16[24,3,80]{2,1,0:T(4,128)(2,1)}, f32[24,3,80]{2,1,0:T(4,128)S(1)}) fusion(bf16[24,3,320]{2,1,0:T(4,128)(2,1)S(1)} %reshape.139, bf16[24,80,320]{2,1,0:T(8,128)(2,1)S(1)} %copy-done, f32[24,3,80]{2,0,1:T(8,128)S(1)} %copy-done.2), kind=kOutput, calls=%fused_computation.23 | convolution fusion | flops 3697920 | bytes 1332480 | tf_op jit(solution)/shard_map/erc,ejc->ejr/dot_general | solution.py:222
  40.2 15.8 %shard_map.97 = bf16[3,4,24,3,80]{4,3,2,1,0:T(4,128)(2,1)} custom-call(bf16[24,3,80]{2,1,0:T(4,128)(2,1)} %get-tuple-element.10.x_ref), custom_call_target="tpu_custom_call" | custom-call | tf_op jit(solution)/shard_map/pallas_call | solution.py:158
  56.0 1.1 %copy.91 = bf16[3,24,3,4,80]{4,3,2,1,0:T(4,128)(2,1)S(1)} copy(bf16[3,24,3,4,80]{4,2,1,3,0:T(4,128)(2,1)} %bitcast.57) | data formatting | bytes 276480 | tf_op jit(solution)/shard_map/reshape | solution.py:178
  57.1 0.3 reshape.140
  57.4 1.1 %gather_fusion.1 = bf16[168,3,320]{2,1,0:T(4,128)(2,1)S(1)} fusion(bf16[72,3,320]{2,1,0:T(4,128)(2,1)S(1)} %reshape.140, s32[1024]{0:T(1024)S(1)} %pad_clamp_fusion), kind=kCustom, calls=%fused_computation.1 | custom fusion | bytes 645792 | tf_op jit(solution)/shard_map/gather | solution.py:215
  58.6 7.5 %fusion.5.x_ref = bf16[24,3,80]{2,1,0:T(4,128)(2,1)} fusion(bf16[24,7,3,320]{3,2,1,0:T(4,128)(2,1)S(1)} %bitcast.53, bf16[24,7,80,320]{3,2,1,0:T(8,128)(2,1)} %param.10, f32[24,3,80]{2,0,1:T(8,128)S(1)} %copy-done.3, f32[24,3,80]{2,1,0:T(4,128)S(1)} %get-tuple-element.11, f32[24]{0:T(128)S(1)} %copy-done.4), kind=kOutput, calls=%fused_computation.13 | convolution fusion | flops 25827840 | bytes 8981856 | tf_op jit(solution)/shard_map/ekrc,ekjc->ejr/dot_general | solution.py:216
  66.1 0.0 copy-start.1
  66.1 5.5 %shard_map.98 = bf16[4,24,3,80]{3,2,1,0:T(4,128)(2,1)} custom-call(bf16[24,3,80]{2,1,0:T(4,128)(2,1)} %fusion.5.x_ref), custom_call_target="tpu_custom_call" | custom-call | tf_op jit(solution)/shard_map/pallas_call | solution.py:158
  71.6 0.9 copy.93
  72.5 0.1 reshape.141
  72.7 0.6 convolution_add_fusion
  73.3 0.6 copy.85
  73.9 0.0 copy-done.1
  73.9 0.2 convolution_negate_fusion
  74.2 0.2 copy.80
  74.3 0.1 reshape.106
  74.5 0.1 copy.81
  74.6 0.1 reshape.129
  74.7 0.3 copy.82
  75.0 9.0 %scatter_custom_fusion = f32[2304,9]{1,0:T(8,128)S(1)} fusion(s32[1536]{0:T(1024)S(1)} %reshape.127, f32[1536,9]{1,0:T(8,128)S(1)} %copy.82, f32[]{:T(128)} %constant.18.clone.1), kind=kCustom, calls=%fused_computation.14 | custom fusion | flops 13824 | bytes 82948 | tf_op jit(solution)/shard_map/scatter-add | solution.py:233
  84.0 1.1 %copy.84 = f32[9,3,4,192]{3,0,2,1:T(8,128)} copy(f32[9,3,4,192]{0,3,2,1:T(8,128)S(1)} %bitcast.52) | data formatting | bytes 165888 | tf_op jit(solution)/shard_map/reshape | solution.py:235
  85.2 13.3 %shard_map.99 = f32[9,192]{1,0:T(8,128)} custom-call(f32[3,4,9,192]{3,2,1,0:T(8,128)} %bitcast.58), custom_call_target="tpu_custom_call" | custom-call | tf_op jit(solution)/shard_map/pallas_call | solution.py:158
  98.5 1.3 %copy.107 = f32[9,192]{1,0:T(8,128)} copy(f32[9,192]{1,0:T(8,128)} %shard_map.99) | data formatting | bytes 13824
  (3 shorter events, 0.0 us)
Async XLA Ops:
  0.6 38.4 %copy-start = (bf16[24,80,320]{2,1,0:T(8,128)(2,1)S(1)}, bf16[24,80,320]{2,1,0:T(8,128)(2,1)}, u32[]{:S(2)}) copy-start(bf16[24,80,320]{2,1,0:T(8,128)(2,1)} %param.11) | copy-start | bytes 3686404
  0.6 24.0 %copy-start.2 = (f32[24,3,80]{2,0,1:T(8,128)S(1)}, f32[24,3,80]{2,0,1:T(8,128)}, u32[]{:S(2)}) copy-start(f32[24,3,80]{2,0,1:T(8,128)} %param.8) | copy-start | bytes 69124
  0.7 24.0 %copy-start.4 = (f32[24]{0:T(128)S(1)}, f32[24]{0:T(128)}, u32[]{:S(2)}) copy-start(f32[24]{0:T(128)} %param.13) | copy-start | bytes 292
  0.7 24.0 %copy-start.3 = (f32[24,3,80]{2,0,1:T(8,128)S(1)}, f32[24,3,80]{2,0,1:T(8,128)}, u32[]{:S(2)}) copy-start(f32[24,3,80]{2,0,1:T(8,128)} %param.9) | copy-start | bytes 69124
  66.1 7.9 %copy-start.1 = (bf16[24,80,192]{2,1,0:T(8,128)(2,1)S(1)}, bf16[24,80,192]{2,1,0:T(8,128)(2,1)}, u32[]{:S(2)}) copy-start(bf16[24,80,192]{2,1,0:T(8,128)(2,1)} %param.14) | copy-start | bytes 2211844

commit v2 on v1

--- a/solution.py
+++ b/solution.py
@@ -192,6 +192,174 @@
     )
 
 
+LANES = 128
+
+
+def _sweeps_kernel(
+    adj_ref, rs_ref, shift_ref, slot_ref, jac_hbm, inv_ref, out_ref,
+    jac_v, send_a, halo, send_r, full_r, upd, jac_sem, hs_send, hs_recv, bk_send, bk_recv,
+):
+    d, b = lax.axis_index("dom"), lax.axis_index("blk")
+    nd, nb = lax.axis_size("dom"), lax.axis_size("blk")
+    rows = adj_ref.shape[0]
+    elems = slot_ref.shape[0]
+    faces = slot_ref.shape[1]
+    partners = _halo_partners(nb)
+
+    def in_range(i):
+        return (i >= 0) & (i < nd)
+
+    _barrier(partners, in_range, d, b, nb)
+    jac_copy = pltpu.make_async_copy(jac_hbm, jac_v, jac_sem)
+    jac_copy.start()
+    lane = lax.broadcasted_iota(jnp.int32, (rows, LANES), 1)
+    wide_lane = lax.broadcasted_iota(jnp.int32, (halo.shape[2], 2 * LANES), 1)
+    own_rows = pl.ds(pl.multiple_of(b * rows, 16), rows)
+    adjoint = adj_ref[...]
+    for sweep in range(SWEEPS):
+        send_a[sweep] = adjoint.astype(jnp.bfloat16)
+
+        def halo_copy(delta, m, sweep=sweep):
+            return pltpu.make_async_remote_copy(
+                src_ref=send_a.at[sweep],
+                dst_ref=halo.at[sweep, 1 - delta, own_rows],
+                send_sem=hs_send.at[sweep, delta + 1, m],
+                recv_sem=hs_recv.at[sweep, 1 - delta, b],
+                device_id=(d + delta, (b + m) % nb),
+                device_id_type=MESH,
+            )
+
+        for delta, m in partners:
+            pl.when(in_range(d + delta))(lambda delta=delta, m=m: halo_copy(delta, m).start())
+        halo[sweep, 1, own_rows] = send_a[sweep]
+        for side in (-1, 1):
+            @pl.when(jnp.logical_not(in_range(d + side)))
+            def _(side=side, sweep=sweep):
+                halo[sweep, 1 + side] = jnp.zeros(halo.shape[2:], halo.dtype)
+        for delta, m in partners:
+            pl.when(in_range(d + delta))(lambda delta=delta, m=m: halo_copy(delta, m).wait_send())
+        for delta, m in partners:
+            p, src_b = 1 + delta, (b + m) % nb
+
+            @pl.when(in_range(d + delta))
+            def _(p=p, src_b=src_b, sweep=sweep):
+                pltpu.make_async_remote_copy(
+                    src_ref=send_a.at[sweep],
+                    dst_ref=halo.at[sweep, p, pl.ds(pl.multiple_of(src_b * rows, 16), rows)],
+                    send_sem=hs_send.at[sweep, p, 0],
+                    recv_sem=hs_recv.at[sweep, p, src_b],
+                    device_id=(d + p - 1, src_b),
+                    device_id_type=MESH,
+                ).wait_recv()
+
+        stride = elems * RHS
+        combined = jnp.zeros((halo.shape[2], 2 * LANES), jnp.float32)
+        for p in range(3):
+            part = halo[sweep, p].astype(jnp.float32)
+            part = jnp.concatenate([part, jnp.zeros_like(part)], axis=1)
+            if p:
+                part = pltpu.roll(part, p * stride, 1)
+            combined = jnp.where(
+                (wide_lane >= p * stride) & (wide_lane < (p + 1) * stride), part, combined
+            )
+        candidates = combined.astype(jnp.bfloat16)
+        if sweep == 0:
+            jac_copy.wait()
+
+        def element(e, product, candidates=candidates):
+            big = jnp.dot(jac_v[e], candidates, preferred_element_type=jnp.float32)
+            acc = jnp.zeros((rows, 2 * LANES), jnp.float32)
+            for k in range(faces + 1):
+                slot = elems + e if k == 0 else slot_ref[e, k - 1]
+                shift = (RHS * e - RHS * slot + 8 * LANES) % (2 * LANES)
+                acc = acc + pltpu.roll(big[k * rows:(k + 1) * rows], shift, 1)
+            mine = (lane >= RHS * e) & (lane < RHS * e + RHS)
+            return product + jnp.where(mine, acc[:, :LANES], 0.0)
+
+        product = lax.fori_loop(0, elems, element, jnp.zeros((rows, LANES), jnp.float32))
+        image = shift_ref[...] * adjoint + product
+        send_r[sweep] = (rs_ref[...] - image).astype(jnp.bfloat16)
+
+        def blk_copy(m, sweep=sweep):
+            return pltpu.make_async_remote_copy(
+                src_ref=send_r.at[sweep],
+                dst_ref=full_r.at[sweep, own_rows],
+                send_sem=bk_send.at[sweep, m],
+                recv_sem=bk_recv.at[sweep, b],
+                device_id=(d, (b + m) % nb),
+                device_id_type=MESH,
+            )
+
+        for m in range(1, nb):
+            blk_copy(m).start()
+        full_r[sweep, own_rows] = send_r[sweep]
+        for m in range(1, nb):
+            blk_copy(m).wait_send()
+        for m in range(1, nb):
+            src_b = (b + m) % nb
+            pltpu.make_async_remote_copy(
+                src_ref=send_r.at[sweep],
+                dst_ref=full_r.at[sweep, pl.ds(pl.multiple_of(src_b * rows, 16), rows)],
+                send_sem=bk_send.at[sweep, 0],
+                recv_sem=bk_recv.at[sweep, src_b],
+                device_id=(d, src_b),
+                device_id_type=MESH,
+            ).wait_recv()
+        upd[...] = jnp.dot(
+            inv_ref[...], full_r[sweep], preferred_element_type=jnp.float32
+        ).reshape(upd.shape)
+        update = jnp.zeros((rows, LANES), jnp.float32)
+        for e in range(elems):
+            mine = (lane >= RHS * e) & (lane < RHS * e + RHS)
+            update = update + jnp.where(mine, upd[e], 0.0)
+        adjoint = adjoint + update
+    out_ref[...] = adjoint
+
+
+def sweeps(adjoint_start, right_sides, pseudo_shift, slots, jac_blocks, block_inverse, nb):
+    elems, rhs, rows = adjoint_start.shape
+    cols = jac_blocks.shape[-1]
+    faces = jac_blocks.shape[1]
+
+    def transposed(x):
+        x = jnp.transpose(x, (2, 0, 1)).reshape(rows, elems * rhs)
+        return jnp.pad(x, ((0, 0), (0, LANES - elems * rhs)))
+
+    shift = jnp.pad(jnp.repeat(pseudo_shift, rhs), (0, LANES - elems * rhs))[None, :]
+    vmem = pl.BlockSpec(memory_space=pltpu.VMEM)
+    out = pl.pallas_call(
+        _sweeps_kernel,
+        out_shape=jax.ShapeDtypeStruct((rows, LANES), jnp.float32),
+        in_specs=[vmem, vmem, vmem, pl.BlockSpec(memory_space=pltpu.SMEM),
+                  pl.BlockSpec(memory_space=pl.ANY), vmem],
+        out_specs=vmem,
+        scratch_shapes=[
+            pltpu.VMEM((elems, faces * rows, cols), jnp.bfloat16),
+            pltpu.VMEM((SWEEPS, rows, LANES), jnp.bfloat16),
+            pltpu.VMEM((SWEEPS, 3, nb * rows, LANES), jnp.bfloat16),
+            pltpu.VMEM((SWEEPS, rows, LANES), jnp.bfloat16),
+            pltpu.VMEM((SWEEPS, nb * rows, LANES), jnp.bfloat16),
+            pltpu.VMEM((elems, rows, LANES), jnp.float32),
+            pltpu.SemaphoreType.DMA(()),
+            pltpu.SemaphoreType.DMA((SWEEPS, 3, nb)),
+            pltpu.SemaphoreType.DMA((SWEEPS, 3, nb)),
+            pltpu.SemaphoreType.DMA((SWEEPS, nb)),
+            pltpu.SemaphoreType.DMA((SWEEPS, nb)),
+        ],
+        compiler_params=pltpu.CompilerParams(
+            collective_id=0, has_side_effects=True, vmem_limit_bytes=48 * 1024 * 1024
+        ),
+    )(
+        transposed(adjoint_start),
+        transposed(right_sides),
+        shift,
+        slots,
+        jac_blocks.reshape(elems, faces * rows, cols),
+        block_inverse.reshape(elems * rows, cols),
+    )
+    return jnp.transpose(out[:, : elems * rhs].reshape(rows, elems, rhs), (1, 2, 0))
+
+
 def local(
     adjoint_start,
     right_sides,
@@ -205,23 +373,8 @@
     local_count = neighbours.shape[0]
     nb = lax.axis_size("blk")
     part_index = lax.axis_index("dom")
-    first_slot = (part_index - 1) * local_count
-    self_slots = jnp.arange(local_count, dtype=jnp.int32)[:, None] + local_count
-    slots = jnp.concatenate([self_slots, neighbours - first_slot], axis=1)
-    adjoint = adjoint_start
-    for sweep in range(SWEEPS):
-        adj_half = adjoint.astype(jnp.bfloat16)
-        extended = halo_gather(adj_half, nb, collective_id=2 * sweep)
-        picked = extended[slots]
-        product = jnp.einsum(
-            "ekrc,ekjc->ejr", jac_blocks, picked, preferred_element_type=jnp.float32
-        )
-        image = pseudo_shift[:, None, None] * adjoint + product
-        resid_half = (right_sides - image).astype(jnp.bfloat16)
-        resid_full = blk_gather(resid_half, nb, collective_id=2 * sweep + 1)
-        adjoint = adjoint + jnp.einsum(
-            "erc,ejc->ejr", block_inverse, resid_full, preferred_element_type=jnp.float32
-        )
+    slots = neighbours - (part_index - 1) * local_count
+    adjoint = sweeps(adjoint_start, right_sides, pseudo_shift, slots, jac_blocks, block_inverse, nb)
     final_half = adjoint.astype(jnp.bfloat16)
     weighted = -jnp.einsum(
         "ejr,erq->ejq", final_half, shape_partials, preferred_element_type=jnp.float32
@@ -234,7 +387,7 @@
     chunks = jnp.transpose(
         partial_sums.reshape(RHS * 3, 3, nb, NODE_DEV // nb), (1, 2, 0, 3)
     )
-    shape_gradient = node_reduce(chunks, collective_id=2 * SWEEPS)
+    shape_gradient = node_reduce(chunks, collective_id=1)
     return (adjoint, shape_gradient)
 
 

time: 100 us -> 85.6 us (0.86)
  matrix products: 17 us -> 0.24 us
  Pallas kernels: 58.5 us -> 65.6 us
  local copies, waits for them, and re-layouts: 12.1 us -> 8.8 us
  other arithmetic: 11.3 us -> 9.83 us
    pallas_call x0 -> x1, Pallas kernels: none -> 53.2 us  [sweeps(): pl.pallas_call(_sweeps_kernel, out_shape=jax.ShapeDtypeStruct((rows, LANE...]
    pallas_call x5 -> x1, Pallas kernels: 58.5 us -> 12.4 us  [_exchange(): pl.pallas_call(kernel, out_shape=jax.ShapeDtypeStruct(out_shape, x.dtype)...]
    dot_general x4 -> x0, matrix products: 16.8 us -> none  [the longest x2 14.9 us: local(): jnp.einsum('ekrc,ekjc->ejr', jac_blocks, picked, preferred_element_type=j...]
    reshape x8 -> x6, local copies, waits for them, and re-layouts: 5.03 us -> 0.31 us  [the longest x4 0.19 us: transposed(): x = jnp.transpose(x, (2, 0, 1)).reshape(rows, elems * rhs)]
    gather x2 -> x0, local copies, waits for them, and re-layouts: 2.28 us -> none  [local(): picked = extended[slots]]
    unnamed x12 -> x7, local copies, waits for them, and re-layouts: 2 us -> 4.09 us
    transpose x0 -> x2, local copies, waits for them, and re-layouts: none -> 1.57 us  [transposed(): x = jnp.transpose(x, (2, 0, 1)).reshape(rows, elems * rhs)]
where the time goes in v2:
time: 85.6 us; the launch traced here: 85.3 us
  Pallas kernels  65.6 us (77%)
  other arithmetic  9.83 us (11%)
  local copies, waits for them, and re-layouts  8.8 us (10%)
    pallas_call x1, Pallas kernels, sweeps(): pl.pallas_call(_sweeps_kernel, out_shape=jax.ShapeDtypeStruct((rows, LANE...  53.2 us
    pallas_call x1, Pallas kernels, _exchange(): pl.pallas_call(kernel, out_shape=jax.ShapeDtypeStruct(out_shape, x.dtype)...  12.4 us
    scatter-add x1, other arithmetic, local(): partial_sums = jax.ops.segment_sum(values, node_slots, 3 * NODE_DEV).T  9.03 us
    unnamed x7, local copies, waits for them, and re-layouts  4.09 us

profile of v2, /device:TPU:7, one launch (start us, length us, event | category | flops | bytes accessed | tf_op | source)
XLA Modules:
  0.0 85.3 jit_solution(12778111984017415410)
XLA Ops:
  0.6 0.0 copy-start
  0.7 0.8 broadcast_subtract_fusion.1
  1.4 0.1 reshape.42
  1.5 0.8 copy.41
  2.3 0.7 broadcast_in_dim.9
  3.0 0.1 reshape.33
  3.1 0.8 copy.37
  3.9 0.1 copy.38
  4.0 0.8 copy.39
  4.8 0.1 copy.40
  4.9 0.0 copy-start.1
  5.0 1.4 %copy-done.1 = bf16[24,80,320]{2,1,0:T(8,128)(2,1)S(1)} copy-done((bf16[24,80,320]{2,1,0:T(8,128)(2,1)S(1)}, bf16[24,80,320]{2,1,0:T(8,128)(2,1)}, u32[]{:S(2)}) %copy-start.1) | copy-done | bytes 1228824
  6.3 53.2 %shard_map.95 = f32[80,128]{1,0:T(8,128)S(1)} custom-call(f32[80,128]{1,0:T(8,128)S(1)} %pad.11.adj_ref, f32[80,128]{1,0:T(8,128)S(1)} %pad.12.rs_ref, f32[1,128]{1,0:T(1,128)S(1)} %pad_bitcast_fusion.shift_ref, s32[24,6]{1,0:T(8,128)S(1)} %broadcast_subtract_fusion.slot_ref, bf16[24,560,320]{2,1,0:T(8,128)(2,1)} %bitcast.41, bf16[1920,320]{1,0:T(8,128)(2,1)S(1)} %bitcast.39), custom_call_target="tpu_custom_call" | custom-call | tf_op jit(solution)/shard_map/pallas_call | solution.py:330
  59.5 0.1 copy.43
  59.6 0.6 copy.49
  60.2 0.0 copy-done
  60.2 0.2 convolution_negate_fusion
  60.5 0.2 copy.44
  60.7 0.1 reshape.37
  60.8 0.1 copy.45
  60.9 0.1 reshape.44
  61.0 0.3 copy.46
  61.3 9.0 %scatter_custom_fusion = f32[2304,9]{1,0:T(8,128)S(1)} fusion(s32[1536]{0:T(1024)S(1)} %reshape.42, f32[1536,9]{1,0:T(8,128)S(1)} %copy.46, f32[]{:T(128)} %constant.6.clone.1), kind=kCustom, calls=%fused_computation.2 | custom fusion | flops 13824 | bytes 82948 | tf_op jit(solution)/shard_map/scatter-add | solution.py:386
  70.4 1.1 %copy.48 = f32[9,3,4,192]{3,0,2,1:T(8,128)} copy(f32[9,3,4,192]{0,3,2,1:T(8,128)S(1)} %bitcast.42) | data formatting | bytes 165888 | tf_op jit(solution)/shard_map/reshape | solution.py:388
  71.5 12.4 %shard_map.96 = f32[9,192]{1,0:T(8,128)} custom-call(f32[3,4,9,192]{3,2,1,0:T(8,128)} %bitcast.44), custom_call_target="tpu_custom_call" | custom-call | tf_op jit(solution)/shard_map/pallas_call | solution.py:158
  83.9 1.3 %copy.53 = f32[9,192]{1,0:T(8,128)} copy(f32[9,192]{1,0:T(8,128)} %shard_map.96) | data formatting | bytes 13824
  (7 shorter events, 0.1 us)
Async XLA Ops:
  0.6 59.6 %copy-start = (bf16[24,80,192]{2,1,0:T(8,128)(2,1)S(1)}, bf16[24,80,192]{2,1,0:T(8,128)(2,1)}, u32[]{:S(2)}) copy-start(bf16[24,80,192]{2,1,0:T(8,128)(2,1)} %param.14) | copy-start | bytes 2211844
  4.9 1.4 %copy-start.1 = (bf16[24,80,320]{2,1,0:T(8,128)(2,1)S(1)}, bf16[24,80,320]{2,1,0:T(8,128)(2,1)}, u32[]{:S(2)}) copy-start(bf16[24,80,320]{2,1,0:T(8,128)(2,1)} %param.11) | copy-start | bytes 3686404

commit v3 on v2

--- a/solution.py
+++ b/solution.py
@@ -198,28 +198,33 @@
 def _sweeps_kernel(
     adj_ref, rs_ref, shift_ref, slot_ref, jac_hbm, inv_ref, out_ref,
     jac_v, send_a, halo, send_r, full_r, upd, jac_sem, hs_send, hs_recv, bk_send, bk_recv,
+    fw_send,
 ):
     d, b = lax.axis_index("dom"), lax.axis_index("blk")
     nd, nb = lax.axis_size("dom"), lax.axis_size("blk")
     rows = adj_ref.shape[0]
     elems = slot_ref.shape[0]
     faces = slot_ref.shape[1]
-    partners = _halo_partners(nb)
 
     def in_range(i):
         return (i >= 0) & (i < nd)
 
+    partners = [(0, m) for m in range(1, nb)] + [(-1, 0), (1, 0)]
     _barrier(partners, in_range, d, b, nb)
     jac_copy = pltpu.make_async_copy(jac_hbm, jac_v, jac_sem)
     jac_copy.start()
     lane = lax.broadcasted_iota(jnp.int32, (rows, LANES), 1)
     wide_lane = lax.broadcasted_iota(jnp.int32, (halo.shape[2], 2 * LANES), 1)
-    own_rows = pl.ds(pl.multiple_of(b * rows, 16), rows)
+
+    def row_block(i):
+        return pl.ds(pl.multiple_of(i * rows, 16), rows)
+
+    own_rows = row_block(b)
     adjoint = adj_ref[...]
     for sweep in range(SWEEPS):
         send_a[sweep] = adjoint.astype(jnp.bfloat16)
 
-        def halo_copy(delta, m, sweep=sweep):
+        def direct(delta, m, sweep=sweep):
             return pltpu.make_async_remote_copy(
                 src_ref=send_a.at[sweep],
                 dst_ref=halo.at[sweep, 1 - delta, own_rows],
@@ -229,28 +234,54 @@
                 device_id_type=MESH,
             )
 
+        def forward(p, m, sweep=sweep):
+            return pltpu.make_async_remote_copy(
+                src_ref=halo.at[sweep, p, own_rows],
+                dst_ref=halo.at[sweep, p, own_rows],
+                send_sem=fw_send.at[sweep, p // 2, m],
+                recv_sem=hs_recv.at[sweep, p, b],
+                device_id=(d, (b + m) % nb),
+                device_id_type=MESH,
+            )
+
+        def arrival(p, src_b, sweep=sweep):
+            return pltpu.make_async_remote_copy(
+                src_ref=send_a.at[sweep],
+                dst_ref=halo.at[sweep, p, row_block(src_b)],
+                send_sem=hs_send.at[sweep, p, 0],
+                recv_sem=hs_recv.at[sweep, p, src_b],
+                device_id=(d, src_b),
+                device_id_type=MESH,
+            )
+
         for delta, m in partners:
-            pl.when(in_range(d + delta))(lambda delta=delta, m=m: halo_copy(delta, m).start())
+            pl.when(in_range(d + delta))(lambda delta=delta, m=m: direct(delta, m).start())
         halo[sweep, 1, own_rows] = send_a[sweep]
         for side in (-1, 1):
             @pl.when(jnp.logical_not(in_range(d + side)))
             def _(side=side, sweep=sweep):
                 halo[sweep, 1 + side] = jnp.zeros(halo.shape[2:], halo.dtype)
+        for side in (-1, 1):
+            p = 1 + side
+
+            @pl.when(in_range(d + side))
+            def _(p=p):
+                arrival(p, b).wait_recv()
+                for m in range(1, nb):
+                    forward(p, m).start()
         for delta, m in partners:
-            pl.when(in_range(d + delta))(lambda delta=delta, m=m: halo_copy(delta, m).wait_send())
-        for delta, m in partners:
-            p, src_b = 1 + delta, (b + m) % nb
-
-            @pl.when(in_range(d + delta))
-            def _(p=p, src_b=src_b, sweep=sweep):
-                pltpu.make_async_remote_copy(
-                    src_ref=send_a.at[sweep],
-                    dst_ref=halo.at[sweep, p, pl.ds(pl.multiple_of(src_b * rows, 16), rows)],
-                    send_sem=hs_send.at[sweep, p, 0],
-                    recv_sem=hs_recv.at[sweep, p, src_b],
-                    device_id=(d + p - 1, src_b),
-                    device_id_type=MESH,
-                ).wait_recv()
+            pl.when(in_range(d + delta))(lambda delta=delta, m=m: direct(delta, m).wait_send())
+        for m in range(1, nb):
+            arrival(1, (b + m) % nb).wait_recv()
+        for side in (-1, 1):
+            p = 1 + side
+
+            @pl.when(in_range(d + side))
+            def _(p=p):
+                for m in range(1, nb):
+                    forward(p, m).wait_send()
+                for m in range(1, nb):
+                    arrival(p, (b + m) % nb).wait_recv()
 
         stride = elems * RHS
         combined = jnp.zeros((halo.shape[2], 2 * LANES), jnp.float32)
@@ -345,6 +376,7 @@
             pltpu.SemaphoreType.DMA((SWEEPS, 3, nb)),
             pltpu.SemaphoreType.DMA((SWEEPS, nb)),
             pltpu.SemaphoreType.DMA((SWEEPS, nb)),
+            pltpu.SemaphoreType.DMA((SWEEPS, 2, nb)),
         ],
         compiler_params=pltpu.CompilerParams(
             collective_id=0, has_side_effects=True, vmem_limit_bytes=48 * 1024 * 1024

time: 85.6 us -> 86.4 us (level)
  no operation moved by 1% of the time
where the time goes in v3:
time: 86.4 us; the launch traced here: 86.1 us
  Pallas kernels  66.4 us (77%)
  other arithmetic  9.83 us (11%)
  local copies, waits for them, and re-layouts  8.8 us (10%)
    pallas_call x1, Pallas kernels, sweeps(): pl.pallas_call(_sweeps_kernel, out_shape=jax.ShapeDtypeStruct((rows, LANE...  53.9 us
    pallas_call x1, Pallas kernels, _exchange(): pl.pallas_call(kernel, out_shape=jax.ShapeDtypeStruct(out_shape, x.dtype)...  12.5 us
    scatter-add x1, other arithmetic, local(): partial_sums = jax.ops.segment_sum(values, node_slots, 3 * NODE_DEV).T  9.03 us
    unnamed x7, local copies, waits for them, and re-layouts  4.09 us

profile of v3, /device:TPU:7, one launch (start us, length us, event | category | flops | bytes accessed | tf_op | source)
XLA Modules:
  0.0 86.1 jit_solution(18040980926812397597)
XLA Ops:
  0.6 0.0 copy-start
  0.7 0.8 broadcast_subtract_fusion.1
  1.4 0.1 reshape.42
  1.5 0.8 copy.41
  2.3 0.7 broadcast_in_dim.9
  3.0 0.1 reshape.33
  3.1 0.8 copy.37
  3.9 0.1 copy.38
  4.0 0.8 copy.39
  4.8 0.1 copy.40
  4.9 0.0 copy-start.1
  5.0 1.4 %copy-done.1 = bf16[24,80,320]{2,1,0:T(8,128)(2,1)S(1)} copy-done((bf16[24,80,320]{2,1,0:T(8,128)(2,1)S(1)}, bf16[24,80,320]{2,1,0:T(8,128)(2,1)}, u32[]{:S(2)}) %copy-start.1) | copy-done | bytes 1228824
  6.3 53.9 %shard_map.95 = f32[80,128]{1,0:T(8,128)S(1)} custom-call(f32[80,128]{1,0:T(8,128)S(1)} %pad.11.adj_ref, f32[80,128]{1,0:T(8,128)S(1)} %pad.12.rs_ref, f32[1,128]{1,0:T(1,128)S(1)} %pad_bitcast_fusion.shift_ref, s32[24,6]{1,0:T(8,128)S(1)} %broadcast_subtract_fusion.slot_ref, bf16[24,560,320]{2,1,0:T(8,128)(2,1)} %bitcast.41, bf16[1920,320]{1,0:T(8,128)(2,1)S(1)} %bitcast.39), custom_call_target="tpu_custom_call" | custom-call | tf_op jit(solution)/shard_map/pallas_call | solution.py:361
  60.2 0.1 copy.43
  60.3 0.6 copy.49
  60.9 0.0 copy-done
  60.9 0.2 convolution_negate_fusion
  61.2 0.2 copy.44
  61.3 0.1 reshape.37
  61.5 0.1 copy.45
  61.6 0.1 reshape.44
  61.7 0.3 copy.46
  62.0 9.0 %scatter_custom_fusion = f32[2304,9]{1,0:T(8,128)S(1)} fusion(s32[1536]{0:T(1024)S(1)} %reshape.42, f32[1536,9]{1,0:T(8,128)S(1)} %copy.46, f32[]{:T(128)} %constant.6.clone.1), kind=kCustom, calls=%fused_computation.2 | custom fusion | flops 13824 | bytes 82948 | tf_op jit(solution)/shard_map/scatter-add | solution.py:418
  71.0 1.1 %copy.48 = f32[9,3,4,192]{3,0,2,1:T(8,128)} copy(f32[9,3,4,192]{0,3,2,1:T(8,128)S(1)} %bitcast.42) | data formatting | bytes 165888 | tf_op jit(solution)/shard_map/reshape | solution.py:420
  72.2 12.5 %shard_map.96 = f32[9,192]{1,0:T(8,128)} custom-call(f32[3,4,9,192]{3,2,1,0:T(8,128)} %bitcast.44), custom_call_target="tpu_custom_call" | custom-call | tf_op jit(solution)/shard_map/pallas_call | solution.py:158
  84.7 1.3 %copy.53 = f32[9,192]{1,0:T(8,128)} copy(f32[9,192]{1,0:T(8,128)} %shard_map.96) | data formatting | bytes 13824
  (7 shorter events, 0.1 us)
Async XLA Ops:
  0.6 60.3 %copy-start = (bf16[24,80,192]{2,1,0:T(8,128)(2,1)S(1)}, bf16[24,80,192]{2,1,0:T(8,128)(2,1)}, u32[]{:S(2)}) copy-start(bf16[24,80,192]{2,1,0:T(8,128)(2,1)} %param.14) | copy-start | bytes 2211844
  4.9 1.4 %copy-start.1 = (bf16[24,80,320]{2,1,0:T(8,128)(2,1)S(1)}, bf16[24,80,320]{2,1,0:T(8,128)(2,1)}, u32[]{:S(2)}) copy-start(bf16[24,80,320]{2,1,0:T(8,128)(2,1)} %param.11) | copy-start | bytes 3686404

commit v4 on v3

--- a/solution.py
+++ b/solution.py
@@ -196,15 +196,15 @@
 
 
 def _sweeps_kernel(
-    adj_ref, rs_ref, shift_ref, slot_ref, jac_hbm, inv_ref, out_ref,
-    jac_v, send_a, halo, send_r, full_r, upd, jac_sem, hs_send, hs_recv, bk_send, bk_recv,
+    adj_ref, rs_ref, shift_ref, target_ref, jac_hbm, inv_ref, out_ref,
+    jac_v, select, send_a, halo, send_r, full_r, upd, jac_sem, hs_send, hs_recv, bk_send, bk_recv,
     fw_send,
 ):
     d, b = lax.axis_index("dom"), lax.axis_index("blk")
     nd, nb = lax.axis_size("dom"), lax.axis_size("blk")
     rows = adj_ref.shape[0]
-    elems = slot_ref.shape[0]
-    faces = slot_ref.shape[1]
+    elems = jac_v.shape[0]
+    faces = jac_v.shape[1]
 
     def in_range(i):
         return (i >= 0) & (i < nd)
@@ -214,7 +214,9 @@
     jac_copy = pltpu.make_async_copy(jac_hbm, jac_v, jac_sem)
     jac_copy.start()
     lane = lax.broadcasted_iota(jnp.int32, (rows, LANES), 1)
-    wide_lane = lax.broadcasted_iota(jnp.int32, (halo.shape[2], 2 * LANES), 1)
+    cand_row = lax.broadcasted_iota(jnp.int32, (3 * LANES, LANES), 0)
+    for k in range(faces):
+        select[k] = (cand_row == target_ref[pl.ds(k, 1), :]).astype(jnp.bfloat16)
 
     def row_block(i):
         return pl.ds(pl.multiple_of(i * rows, 16), rows)
@@ -283,31 +285,22 @@
                 for m in range(1, nb):
                     arrival(p, (b + m) % nb).wait_recv()
 
-        stride = elems * RHS
-        combined = jnp.zeros((halo.shape[2], 2 * LANES), jnp.float32)
-        for p in range(3):
-            part = halo[sweep, p].astype(jnp.float32)
-            part = jnp.concatenate([part, jnp.zeros_like(part)], axis=1)
-            if p:
-                part = pltpu.roll(part, p * stride, 1)
-            combined = jnp.where(
-                (wide_lane >= p * stride) & (wide_lane < (p + 1) * stride), part, combined
-            )
-        candidates = combined.astype(jnp.bfloat16)
+        candidates = jnp.concatenate([halo[sweep, p] for p in range(3)], axis=1)
         if sweep == 0:
             jac_copy.wait()
-
-        def element(e, product, candidates=candidates):
-            big = jnp.dot(jac_v[e], candidates, preferred_element_type=jnp.float32)
-            acc = jnp.zeros((rows, 2 * LANES), jnp.float32)
-            for k in range(faces + 1):
-                slot = elems + e if k == 0 else slot_ref[e, k - 1]
-                shift = (RHS * e - RHS * slot + 8 * LANES) % (2 * LANES)
-                acc = acc + pltpu.roll(big[k * rows:(k + 1) * rows], shift, 1)
+        acc = jnp.zeros((elems * rows, LANES), jnp.float32)
+        for k in range(faces):
+            picked = jnp.dot(candidates, select[k], preferred_element_type=jnp.float32)
+            acc = acc + jnp.dot(
+                jac_v[:, k].reshape(elems * rows, -1),
+                picked.astype(jnp.bfloat16),
+                preferred_element_type=jnp.float32,
+            )
+        upd[...] = acc.reshape(upd.shape)
+        product = jnp.zeros((rows, LANES), jnp.float32)
+        for e in range(elems):
             mine = (lane >= RHS * e) & (lane < RHS * e + RHS)
-            return product + jnp.where(mine, acc[:, :LANES], 0.0)
-
-        product = lax.fori_loop(0, elems, element, jnp.zeros((rows, LANES), jnp.float32))
+            product = product + jnp.where(mine, upd[e], 0.0)
         image = shift_ref[...] * adjoint + product
         send_r[sweep] = (rs_ref[...] - image).astype(jnp.bfloat16)
 
@@ -357,15 +350,19 @@
         return jnp.pad(x, ((0, 0), (0, LANES - elems * rhs)))
 
     shift = jnp.pad(jnp.repeat(pseudo_shift, rhs), (0, LANES - elems * rhs))[None, :]
+    part, within = slots // elems, slots % elems
+    lanes = (part * LANES + within * rhs)[:, :, None] + jnp.arange(rhs, dtype=jnp.int32)
+    target = jnp.transpose(lanes, (1, 0, 2)).reshape(faces, elems * rhs)
+    target = jnp.pad(target, ((0, 8 - faces), (0, LANES - elems * rhs)), constant_values=-1)
     vmem = pl.BlockSpec(memory_space=pltpu.VMEM)
     out = pl.pallas_call(
         _sweeps_kernel,
         out_shape=jax.ShapeDtypeStruct((rows, LANES), jnp.float32),
-        in_specs=[vmem, vmem, vmem, pl.BlockSpec(memory_space=pltpu.SMEM),
-                  pl.BlockSpec(memory_space=pl.ANY), vmem],
+        in_specs=[vmem, vmem, vmem, vmem, pl.BlockSpec(memory_space=pl.ANY), vmem],
         out_specs=vmem,
         scratch_shapes=[
-            pltpu.VMEM((elems, faces * rows, cols), jnp.bfloat16),
+            pltpu.VMEM((elems, faces, rows, cols), jnp.bfloat16),
+            pltpu.VMEM((faces, 3 * LANES, LANES), jnp.bfloat16),
             pltpu.VMEM((SWEEPS, rows, LANES), jnp.bfloat16),
             pltpu.VMEM((SWEEPS, 3, nb * rows, LANES), jnp.bfloat16),
             pltpu.VMEM((SWEEPS, rows, LANES), jnp.bfloat16),
@@ -385,8 +382,8 @@
         transposed(adjoint_start),
         transposed(right_sides),
         shift,
-        slots,
-        jac_blocks.reshape(elems, faces * rows, cols),
+        target,
+        jac_blocks,
         block_inverse.reshape(elems * rows, cols),
     )
     return jnp.transpose(out[:, : elems * rhs].reshape(rows, elems, rhs), (1, 2, 0))
@@ -405,7 +402,8 @@
     local_count = neighbours.shape[0]
     nb = lax.axis_size("blk")
     part_index = lax.axis_index("dom")
-    slots = neighbours - (part_index - 1) * local_count
+    own = jnp.arange(local_count, dtype=jnp.int32)[:, None] + local_count
+    slots = jnp.concatenate([own, neighbours - (part_index - 1) * local_count], axis=1)
     adjoint = sweeps(adjoint_start, right_sides, pseudo_shift, slots, jac_blocks, block_inverse, nb)
     final_half = adjoint.astype(jnp.bfloat16)
     weighted = -jnp.einsum(

time: 86.4 us -> 75.5 us (0.87)
  Pallas kernels: 66.4 us -> 55.1 us
    pallas_call x1, Pallas kernels: 53.9 us -> 42.6 us  [sweeps(): pl.pallas_call(_sweeps_kernel, out_shape=jax.ShapeDtypeStruct((rows, LANE...]
    unnamed x7 -> x6, local copies, waits for them, and re-layouts: 4.09 us -> 3.32 us
where the time goes in v4:
time: 75.5 us; the launch traced here: 75.1 us
  Pallas kernels  55.1 us (73%)
  other arithmetic  10.6 us (14%)
  local copies, waits for them, and re-layouts  8.33 us (11%)
  between operations  0.81 us (1%)
    pallas_call x1, Pallas kernels, sweeps(): pl.pallas_call(_sweeps_kernel, out_shape=jax.ShapeDtypeStruct((rows, LANE...  42.6 us
    pallas_call x1, Pallas kernels, _exchange(): pl.pallas_call(kernel, out_shape=jax.ShapeDtypeStruct(out_shape, x.dtype)...  12.5 us
    scatter-add x1, other arithmetic, local(): partial_sums = jax.ops.segment_sum(values, node_slots, 3 * NODE_DEV).T  9.03 us
    unnamed x6, local copies, waits for them, and re-layouts  3.32 us
    transpose x2, local copies, waits for them, and re-layouts, transposed(): x = jnp.transpose(x, (2, 0, 1)).reshape(rows, elems * rhs)  1.57 us

profile of v4, /device:TPU:7, one launch (start us, length us, event | category | flops | bytes accessed | tf_op | source)
XLA Modules:
  0.0 75.1 jit_solution(17747514476775164900)
XLA Ops:
  0.6 0.0 copy-start
  0.7 0.8 %broadcast_subtract_fusion.1 = s32[24,6]{0,1:T(8,128)S(1)} fusion(s32[24,6]{0,1:T(8,128)} %param.12, s32[]{:T(128)S(6)} %mul.26), kind=kLoop, calls=%fused_computation.17 | loop fusion | flops 144 | bytes 1156 | tf_op jit(solution)/shard_map/sub | solution.py:406
  1.5 0.1 copy.29
  1.5 0.7 broadcast_subtract_fusion
  2.3 0.1 reshape.97
  2.3 0.7 broadcast_in_dim.12
  3.1 0.1 reshape.89
  3.2 0.1 add.78
  3.3 0.1 copy.30
  3.4 0.8 %copy.25 = f32[80,24,3]{0,2,1:T(4,128)S(1)} copy(f32[80,24,3]{0,1,2:T(8,128)} %bitcast.48) | data formatting | bytes 46080 | tf_op jit(solution)/shard_map/transpose | solution.py:349
  4.2 0.1 copy.26
  4.3 0.8 %copy.27 = f32[80,24,3]{0,2,1:T(4,128)S(1)} copy(f32[80,24,3]{0,1,2:T(8,128)} %bitcast.49) | data formatting | bytes 46080 | tf_op jit(solution)/shard_map/transpose | solution.py:349
  5.1 0.1 copy.28
  5.2 0.0 copy-start.1
  5.2 1.4 %copy-done.1 = bf16[24,80,320]{2,1,0:T(8,128)(2,1)S(1)} copy-done((bf16[24,80,320]{2,1,0:T(8,128)(2,1)S(1)}, bf16[24,80,320]{2,1,0:T(8,128)(2,1)}, u32[]{:S(2)}) %copy-start.1) | copy-done | bytes 1228824
  6.6 42.6 %shard_map.95 = f32[80,128]{1,0:T(8,128)S(1)} custom-call(f32[80,128]{1,0:T(8,128)S(1)} %pad.15.adj_ref, f32[80,128]{1,0:T(8,128)S(1)} %pad.16.rs_ref, f32[1,128]{1,0:T(1,128)S(1)} %pad_bitcast_fusion.shift_ref, s32[8,128]{1,0:T(8,128)S(1)} %pad.18.target_ref, bf16[24,7,80,320]{3,2,1,0:T(8,128)(2,1)} %jac_hbm.1, bf16[1920,320]{1,0:T(8,128)(2,1)S(1)} %bitcast.42), custom_call_target="tpu_custom_call" | custom-call | tf_op jit(solution)/shard_map/pallas_call | solution.py:358
  49.2 0.1 copy.31
  49.3 0.6 copy.37
  50.0 0.0 copy-done
  50.0 0.2 convolution_negate_fusion
  50.2 0.2 copy.32
  50.4 0.1 reshape.92
  50.5 0.1 copy.33
  50.6 0.1 reshape.99
  50.7 0.3 copy.34
  51.0 9.0 %scatter_custom_fusion = f32[2304,9]{1,0:T(8,128)S(1)} fusion(s32[1536]{0:T(1024)S(1)} %reshape.97, f32[1536,9]{1,0:T(8,128)S(1)} %copy.34, f32[]{:T(128)} %constant.16.clone.1), kind=kCustom, calls=%fused_computation.2 | custom fusion | flops 13824 | bytes 82948 | tf_op jit(solution)/shard_map/scatter-add | solution.py:416
  60.1 1.1 %copy.36 = f32[9,3,4,192]{3,0,2,1:T(8,128)} copy(f32[9,3,4,192]{0,3,2,1:T(8,128)S(1)} %bitcast.44) | data formatting | bytes 165888 | tf_op jit(solution)/shard_map/reshape | solution.py:418
  61.2 12.5 %shard_map.96 = f32[9,192]{1,0:T(8,128)} custom-call(f32[3,4,9,192]{3,2,1,0:T(8,128)} %bitcast.46), custom_call_target="tpu_custom_call" | custom-call | tf_op jit(solution)/shard_map/pallas_call | solution.py:158
  73.8 1.3 %copy.41 = f32[9,192]{1,0:T(8,128)} copy(f32[9,192]{1,0:T(8,128)} %shard_map.96) | data formatting | bytes 13824
  (13 shorter events, 0.2 us)
Async XLA Ops:
  0.6 49.3 %copy-start = (bf16[24,80,192]{2,1,0:T(8,128)(2,1)S(1)}, bf16[24,80,192]{2,1,0:T(8,128)(2,1)}, u32[]{:S(2)}) copy-start(bf16[24,80,192]{2,1,0:T(8,128)(2,1)} %param.14) | copy-start | bytes 2211844
  5.2 1.4 %copy-start.1 = (bf16[24,80,320]{2,1,0:T(8,128)(2,1)S(1)}, bf16[24,80,320]{2,1,0:T(8,128)(2,1)}, u32[]{:S(2)}) copy-start(bf16[24,80,320]{2,1,0:T(8,128)(2,1)} %param.11) | copy-start | bytes 3686404

commit v5 on v4

--- a/solution.py
+++ b/solution.py
@@ -196,9 +196,9 @@
 
 
 def _sweeps_kernel(
-    adj_ref, rs_ref, shift_ref, target_ref, jac_hbm, inv_ref, out_ref,
+    adj_ref, rs_ref, shift_ref, target_ref, jac_hbm, inv_ref, shape_ref, out_ref, wsum_ref,
     jac_v, select, send_a, halo, send_r, full_r, upd, jac_sem, hs_send, hs_recv, bk_send, bk_recv,
-    fw_send,
+    fw_send, wpart, ws_send, ws_recv,
 ):
     d, b = lax.axis_index("dom"), lax.axis_index("blk")
     nd, nb = lax.axis_size("dom"), lax.axis_size("blk")
@@ -339,8 +339,56 @@
         adjoint = adjoint + update
     out_ref[...] = adjoint
 
-
-def sweeps(adjoint_start, right_sides, pseudo_shift, slots, jac_blocks, block_inverse, nb):
+    square = jnp.concatenate([adjoint, jnp.zeros((LANES - rows, LANES), jnp.float32)], axis=0)
+    final_half = jnp.transpose(square)[:, :rows].astype(jnp.bfloat16)
+    row = lax.broadcasted_iota(jnp.int32, (LANES, shape_ref.shape[2]), 0)
+    weighted = jnp.zeros((LANES, shape_ref.shape[2]), jnp.float32)
+    for e in range(elems):
+        part = jnp.dot(final_half, shape_ref[e], preferred_element_type=jnp.float32)
+        weighted = weighted + jnp.where((row >= RHS * e) & (row < RHS * e + RHS), part, 0.0)
+    wpart[pl.ds(0, LANES)] = -weighted
+    chunk = wsum_ref.shape[0]
+    owners = pl.cdiv(elems * RHS, chunk)
+
+    def wcopy(c, src_b):
+        return pltpu.make_async_remote_copy(
+            src_ref=wpart.at[pl.ds(c * chunk, chunk)],
+            dst_ref=wpart.at[pl.ds(LANES + src_b * chunk, chunk)],
+            send_sem=ws_send.at[c],
+            recv_sem=ws_recv.at[src_b],
+            device_id=(d, c),
+            device_id_type=MESH,
+        )
+
+    for m in range(1, nb):
+        c = (b + m) % nb
+        pl.when(c < owners)(lambda c=c: wcopy(c, b).start())
+    for m in range(1, nb):
+        c = (b + m) % nb
+        pl.when(c < owners)(lambda c=c: wcopy(c, b).wait_send())
+    total = jnp.zeros(wsum_ref.shape, jnp.float32)
+    for m in range(1, nb):
+        src_b = (b + m) % nb
+
+        @pl.when(b < owners)
+        def _(src_b=src_b):
+            wcopy(b, src_b).wait_recv()
+
+    @pl.when(b < owners)
+    def _():
+        acc = wpart[pl.ds(pl.multiple_of(b * chunk, 8), chunk)]
+        for m in range(1, nb):
+            src_b = (b + m) % nb
+            acc = acc + wpart[pl.ds(pl.multiple_of(LANES + src_b * chunk, 8), chunk)]
+        wsum_ref[...] = acc
+
+    @pl.when(b >= owners)
+    def _():
+        wsum_ref[...] = jnp.zeros(wsum_ref.shape, jnp.float32)
+
+
+def sweeps(adjoint_start, right_sides, pseudo_shift, slots, jac_blocks, block_inverse,
+           shape_partials, nb):
     elems, rhs, rows = adjoint_start.shape
     cols = jac_blocks.shape[-1]
     faces = jac_blocks.shape[1]
@@ -355,11 +403,15 @@
     target = jnp.transpose(lanes, (1, 0, 2)).reshape(faces, elems * rhs)
     target = jnp.pad(target, ((0, 8 - faces), (0, LANES - elems * rhs)), constant_values=-1)
     vmem = pl.BlockSpec(memory_space=pltpu.VMEM)
-    out = pl.pallas_call(
+    chunk = 8 * rhs
+    out, wsum = pl.pallas_call(
         _sweeps_kernel,
-        out_shape=jax.ShapeDtypeStruct((rows, LANES), jnp.float32),
-        in_specs=[vmem, vmem, vmem, vmem, pl.BlockSpec(memory_space=pl.ANY), vmem],
-        out_specs=vmem,
+        out_shape=(
+            jax.ShapeDtypeStruct((rows, LANES), jnp.float32),
+            jax.ShapeDtypeStruct((chunk, shape_partials.shape[2]), jnp.float32),
+        ),
+        in_specs=[vmem, vmem, vmem, vmem, pl.BlockSpec(memory_space=pl.ANY), vmem, vmem],
+        out_specs=(vmem, vmem),
         scratch_shapes=[
             pltpu.VMEM((elems, faces, rows, cols), jnp.bfloat16),
             pltpu.VMEM((faces, 3 * LANES, LANES), jnp.bfloat16),
@@ -374,6 +426,9 @@
             pltpu.SemaphoreType.DMA((SWEEPS, nb)),
             pltpu.SemaphoreType.DMA((SWEEPS, nb)),
             pltpu.SemaphoreType.DMA((SWEEPS, 2, nb)),
+            pltpu.VMEM((LANES + nb * chunk, shape_partials.shape[2]), jnp.float32),
+            pltpu.SemaphoreType.DMA((nb,)),
+            pltpu.SemaphoreType.DMA((nb,)),
         ],
         compiler_params=pltpu.CompilerParams(
             collective_id=0, has_side_effects=True, vmem_limit_bytes=48 * 1024 * 1024
@@ -385,8 +440,10 @@
         target,
         jac_blocks,
         block_inverse.reshape(elems * rows, cols),
-    )
-    return jnp.transpose(out[:, : elems * rhs].reshape(rows, elems, rhs), (1, 2, 0))
+        shape_partials,
+    )
+    adjoint = jnp.transpose(out[:, : elems * rhs].reshape(rows, elems, rhs), (1, 2, 0))
+    return adjoint, wsum
 
 
 def local(
@@ -404,15 +461,19 @@
     part_index = lax.axis_index("dom")
     own = jnp.arange(local_count, dtype=jnp.int32)[:, None] + local_count
     slots = jnp.concatenate([own, neighbours - (part_index - 1) * local_count], axis=1)
-    adjoint = sweeps(adjoint_start, right_sides, pseudo_shift, slots, jac_blocks, block_inverse, nb)
-    final_half = adjoint.astype(jnp.bfloat16)
-    weighted = -jnp.einsum(
-        "ejr,erq->ejq", final_half, shape_partials, preferred_element_type=jnp.float32
+    adjoint, wsum = sweeps(
+        adjoint_start, right_sides, pseudo_shift, slots, jac_blocks, block_inverse,
+        shape_partials, nb,
     )
     node_width = node_ids.shape[1]
-    weighted = weighted.reshape(local_count, RHS, node_width, 3)
-    values = jnp.transpose(weighted, (0, 2, 1, 3)).reshape(local_count * node_width, RHS * 3)
-    node_slots = (node_ids - (part_index - 1) * NODE_DEV).reshape(-1)
+    chunk_elems = wsum.shape[0] // RHS
+    values = wsum.reshape(chunk_elems, RHS, node_width, 3)
+    values = jnp.transpose(values, (0, 2, 1, 3)).reshape(chunk_elems * node_width, RHS * 3)
+    my_nodes = lax.dynamic_slice_in_dim(
+        node_ids, jnp.minimum(lax.axis_index("blk") * chunk_elems, local_count - chunk_elems),
+        chunk_elems,
+    )
+    node_slots = (my_nodes - (part_index - 1) * NODE_DEV).reshape(-1)
     partial_sums = jax.ops.segment_sum(values, node_slots, 3 * NODE_DEV).T
     chunks = jnp.transpose(
         partial_sums.reshape(RHS * 3, 3, nb, NODE_DEV // nb), (1, 2, 0, 3)

time: 75.5 us -> 73.4 us (0.972)
  other arithmetic: 10.6 us -> 4.06 us
  Pallas kernels: 55.1 us -> 59.4 us
    scatter-add x1, other arithmetic: 9.03 us -> 2.54 us  [local(): partial_sums = jax.ops.segment_sum(values, node_slots, 3 * NODE_DEV).T]
    pallas_call x1, Pallas kernels: 42.6 us -> 45.8 us  [sweeps(): pl.pallas_call(_sweeps_kernel, out_shape=(jax.ShapeDtypeStruct((rows, LAN...]
    pallas_call x1, Pallas kernels: 12.5 us -> 13.5 us  [_exchange(): pl.pallas_call(kernel, out_shape=jax.ShapeDtypeStruct(out_shape, x.dtype)...]
where the time goes in v5:
time: 73.4 us; the launch traced here: 73 us
  Pallas kernels  59.4 us (81%)
  local copies, waits for them, and re-layouts  8.8 us (12%)
  other arithmetic  4.06 us (6%)
  between operations  0.81 us (1%)
    pallas_call x1, Pallas kernels, sweeps(): pl.pallas_call(_sweeps_kernel, out_shape=(jax.ShapeDtypeStruct((rows, LAN...  45.8 us
    pallas_call x1, Pallas kernels, _exchange(): pl.pallas_call(kernel, out_shape=jax.ShapeDtypeStruct(out_shape, x.dtype)...  13.5 us
    unnamed x6, local copies, waits for them, and re-layouts  3.32 us
    scatter-add x1, other arithmetic, local(): partial_sums = jax.ops.segment_sum(values, node_slots, 3 * NODE_DEV).T  2.54 us
    transpose x2, local copies, waits for them, and re-layouts, transposed(): x = jnp.transpose(x, (2, 0, 1)).reshape(rows, elems * rhs)  1.57 us

profile of v5, /device:TPU:7, one launch (start us, length us, event | category | flops | bytes accessed | tf_op | source)
XLA Modules:
  0.0 73.0 jit_solution(18366342686405994125)
XLA Ops:
  0.6 0.0 copy-start.1
  0.7 0.8 %dynamic-slice_subtract_fusion = s32[8,64]{1,0:T(8,128)S(1)} fusion(s32[24,64]{1,0:T(8,128)} %param.15, s32[]{:T(128)S(6)} %select_n.25, s32[]{:T(128)S(6)} %mul.35), kind=kLoop, calls=%fused_computation.10 | loop fusion | flops 512 | bytes 4104 | tf_op jit(solution)/shard_map/sub | solution.py:476
  1.5 0.1 reshape.97
  1.5 0.7 broadcast_subtract_fusion
  2.2 0.1 copy.27
  2.3 0.7 broadcast_in_dim.12
  3.1 0.1 reshape.89
  3.2 0.1 add.81
  3.3 0.1 copy.28
  3.4 0.8 %copy.23 = f32[80,24,3]{0,2,1:T(4,128)S(1)} copy(f32[80,24,3]{0,1,2:T(8,128)} %bitcast.32) | data formatting | bytes 46080 | tf_op jit(solution)/shard_map/transpose | solution.py:397
  4.2 0.1 copy.24
  4.3 0.8 %copy.25 = f32[80,24,3]{0,2,1:T(4,128)S(1)} copy(f32[80,24,3]{0,1,2:T(8,128)} %bitcast.33) | data formatting | bytes 46080 | tf_op jit(solution)/shard_map/transpose | solution.py:397
  5.1 0.1 copy.26
  5.2 0.0 copy-done.1
  5.2 0.0 copy-start
  5.3 1.4 %copy-done = bf16[24,80,320]{2,1,0:T(8,128)(2,1)S(1)} copy-done((bf16[24,80,320]{2,1,0:T(8,128)(2,1)S(1)}, bf16[24,80,320]{2,1,0:T(8,128)(2,1)}, u32[]{:S(2)}) %copy-start) | copy-done | bytes 1228824
  6.6 45.8 %shard_map.95 = (f32[80,128]{1,0:T(8,128)S(1)}, f32[24,192]{1,0:T(8,128)S(1)}) custom-call(f32[80,128]{1,0:T(8,128)S(1)} %pad.15.adj_ref, f32[80,128]{1,0:T(8,128)S(1)} %pad.16.rs_ref, f32[1,128]{1,0:T(1,128)S(1)} %pad_bitcast_fusion.shift_ref, s32[8,128]{1,0:T(8,128)S(1)} %pad.18.target_ref, bf16[24,7,80,320]{3,2,1,0:T(8,128)(2,1)} %jac_hbm.1, ...), custom_call_target="tpu_custom_call" | custom-call | tf_op jit(solution)/shard_map/pallas_call | solution.py:407
  52.5 0.1 copy.29
  52.6 0.6 copy.34
  53.2 0.7 %reshape.92 = f32[8,3,64,3]{3,2,1,0:T(8,128)S(1)} reshape(f32[24,192]{1,0:T(8,128)S(1)} %get-tuple-element.5) | data formatting | bytes 36864 | tf_op jit(solution)/shard_map/reshape | solution.py:470
  53.9 0.3 copy.30
  54.2 0.1 reshape.99
  54.3 0.1 copy.31
  54.5 2.5 %scatter_custom_fusion = f32[2304,9]{1,0:T(8,128)S(1)} fusion(s32[512]{0:T(512)S(1)} %reshape.97, f32[512,9]{1,0:T(8,128)S(1)} %copy.31, f32[]{:T(128)} %constant.15.clone.1), kind=kCustom, calls=%fused_computation.1 | custom fusion | flops 4608 | bytes 82948 | tf_op jit(solution)/shard_map/scatter-add | solution.py:477
  57.0 1.1 %copy.33 = f32[9,3,4,192]{3,0,2,1:T(8,128)} copy(f32[9,3,4,192]{0,3,2,1:T(8,128)S(1)} %bitcast.28) | data formatting | bytes 165888 | tf_op jit(solution)/shard_map/reshape | solution.py:479
  58.2 13.5 %shard_map.96 = f32[9,192]{1,0:T(8,128)} custom-call(f32[3,4,9,192]{3,2,1,0:T(8,128)} %bitcast.30), custom_call_target="tpu_custom_call" | custom-call | tf_op jit(solution)/shard_map/pallas_call | solution.py:158
  71.7 1.3 %copy.38 = f32[9,192]{1,0:T(8,128)} copy(f32[9,192]{1,0:T(8,128)} %shard_map.96) | data formatting | bytes 13824
  (13 shorter events, 0.2 us)
Async XLA Ops:
  0.6 4.6 %copy-start.1 = (bf16[24,80,192]{2,1,0:T(8,128)(2,1)S(1)}, bf16[24,80,192]{2,1,0:T(8,128)(2,1)}, u32[]{:S(2)}) copy-start(bf16[24,80,192]{2,1,0:T(8,128)(2,1)} %shape_ref.1) | copy-start | bytes 2211844
  5.2 1.4 %copy-start = (bf16[24,80,320]{2,1,0:T(8,128)(2,1)S(1)}, bf16[24,80,320]{2,1,0:T(8,128)(2,1)}, u32[]{:S(2)}) copy-start(bf16[24,80,320]{2,1,0:T(8,128)(2,1)} %param.11) | copy-start | bytes 3686404

commit v6 on v5

--- a/solution.py
+++ b/solution.py
@@ -196,13 +196,13 @@
 
 
 def _sweeps_kernel(
-    adj_ref, rs_ref, shift_ref, target_ref, jac_hbm, inv_ref, shape_ref, out_ref, wsum_ref,
-    jac_v, select, send_a, halo, send_r, full_r, upd, jac_sem, hs_send, hs_recv, bk_send, bk_recv,
+    start_ref, shift_ref, target_ref, jac_hbm, inv_hbm, shape_hbm, out_ref, wsum_ref,
+    jac_v, inv_ref, shape_ref, select, send_a, halo, send_r, full_r, upd, jac_sem, hs_send, hs_recv, bk_send, bk_recv,
     fw_send, wpart, ws_send, ws_recv,
 ):
     d, b = lax.axis_index("dom"), lax.axis_index("blk")
     nd, nb = lax.axis_size("dom"), lax.axis_size("blk")
-    rows = adj_ref.shape[0]
+    rows = start_ref.shape[1]
     elems = jac_v.shape[0]
     faces = jac_v.shape[1]
 
@@ -211,8 +211,12 @@
 
     partners = [(0, m) for m in range(1, nb)] + [(-1, 0), (1, 0)]
     _barrier(partners, in_range, d, b, nb)
-    jac_copy = pltpu.make_async_copy(jac_hbm, jac_v, jac_sem)
+    jac_copy = pltpu.make_async_copy(jac_hbm, jac_v, jac_sem.at[0])
+    inv_copy = pltpu.make_async_copy(inv_hbm, inv_ref, jac_sem.at[1])
+    shape_copy = pltpu.make_async_copy(shape_hbm, shape_ref, jac_sem.at[2])
     jac_copy.start()
+    inv_copy.start()
+    shape_copy.start()
     lane = lax.broadcasted_iota(jnp.int32, (rows, LANES), 1)
     cand_row = lax.broadcasted_iota(jnp.int32, (3 * LANES, LANES), 0)
     for k in range(faces):
@@ -222,7 +226,7 @@
         return pl.ds(pl.multiple_of(i * rows, 16), rows)
 
     own_rows = row_block(b)
-    adjoint = adj_ref[...]
+    adjoint = start_ref[0]
     for sweep in range(SWEEPS):
         send_a[sweep] = adjoint.astype(jnp.bfloat16)
 
@@ -302,7 +306,7 @@
             mine = (lane >= RHS * e) & (lane < RHS * e + RHS)
             product = product + jnp.where(mine, upd[e], 0.0)
         image = shift_ref[...] * adjoint + product
-        send_r[sweep] = (rs_ref[...] - image).astype(jnp.bfloat16)
+        send_r[sweep] = (start_ref[1] - image).astype(jnp.bfloat16)
 
         def blk_copy(m, sweep=sweep):
             return pltpu.make_async_remote_copy(
@@ -329,6 +333,8 @@
                 device_id=(d, src_b),
                 device_id_type=MESH,
             ).wait_recv()
+        if sweep == 0:
+            inv_copy.wait()
         upd[...] = jnp.dot(
             inv_ref[...], full_r[sweep], preferred_element_type=jnp.float32
         ).reshape(upd.shape)
@@ -340,13 +346,20 @@
     out_ref[...] = adjoint
 
     square = jnp.concatenate([adjoint, jnp.zeros((LANES - rows, LANES), jnp.float32)], axis=0)
-    final_half = jnp.transpose(square)[:, :rows].astype(jnp.bfloat16)
-    row = lax.broadcasted_iota(jnp.int32, (LANES, shape_ref.shape[2]), 0)
-    weighted = jnp.zeros((LANES, shape_ref.shape[2]), jnp.float32)
+    final_f32 = jnp.transpose(square)[:, :rows]
+    window = 16
+    row = lax.broadcasted_iota(jnp.int32, (window, shape_ref.shape[2]), 0)
+    wpart[pl.ds(0, LANES)] = jnp.zeros((LANES, shape_ref.shape[2]), jnp.float32)
+    shape_copy.wait()
     for e in range(elems):
-        part = jnp.dot(final_half, shape_ref[e], preferred_element_type=jnp.float32)
-        weighted = weighted + jnp.where((row >= RHS * e) & (row < RHS * e + RHS), part, 0.0)
-    wpart[pl.ds(0, LANES)] = -weighted
+        low = (RHS * e) // 8 * 8
+        part = jnp.dot(
+            final_f32[low:low + window].astype(jnp.bfloat16),
+            shape_ref[e],
+            preferred_element_type=jnp.float32,
+        )
+        mine = (row + low >= RHS * e) & (row + low < RHS * e + RHS)
+        wpart[pl.ds(low, window)] = wpart[pl.ds(low, window)] - jnp.where(mine, part, 0.0)
     chunk = wsum_ref.shape[0]
     owners = pl.cdiv(elems * RHS, chunk)
 
@@ -394,8 +407,8 @@
     faces = jac_blocks.shape[1]
 
     def transposed(x):
-        x = jnp.transpose(x, (2, 0, 1)).reshape(rows, elems * rhs)
-        return jnp.pad(x, ((0, 0), (0, LANES - elems * rhs)))
+        x = jnp.transpose(x, (0, 3, 1, 2)).reshape(x.shape[0], rows, elems * rhs)
+        return jnp.pad(x, ((0, 0), (0, 0), (0, LANES - elems * rhs)))
 
     shift = jnp.pad(jnp.repeat(pseudo_shift, rhs), (0, LANES - elems * rhs))[None, :]
     part, within = slots // elems, slots % elems
@@ -403,6 +416,7 @@
     target = jnp.transpose(lanes, (1, 0, 2)).reshape(faces, elems * rhs)
     target = jnp.pad(target, ((0, 8 - faces), (0, LANES - elems * rhs)), constant_values=-1)
     vmem = pl.BlockSpec(memory_space=pltpu.VMEM)
+    hbm = pl.BlockSpec(memory_space=pl.ANY)
     chunk = 8 * rhs
     out, wsum = pl.pallas_call(
         _sweeps_kernel,
@@ -410,17 +424,19 @@
             jax.ShapeDtypeStruct((rows, LANES), jnp.float32),
             jax.ShapeDtypeStruct((chunk, shape_partials.shape[2]), jnp.float32),
         ),
-        in_specs=[vmem, vmem, vmem, vmem, pl.BlockSpec(memory_space=pl.ANY), vmem, vmem],
+        in_specs=[vmem, vmem, vmem, hbm, hbm, hbm],
         out_specs=(vmem, vmem),
         scratch_shapes=[
             pltpu.VMEM((elems, faces, rows, cols), jnp.bfloat16),
+            pltpu.VMEM((elems * rows, cols), jnp.bfloat16),
+            pltpu.VMEM(shape_partials.shape, shape_partials.dtype),
             pltpu.VMEM((faces, 3 * LANES, LANES), jnp.bfloat16),
             pltpu.VMEM((SWEEPS, rows, LANES), jnp.bfloat16),
             pltpu.VMEM((SWEEPS, 3, nb * rows, LANES), jnp.bfloat16),
             pltpu.VMEM((SWEEPS, rows, LANES), jnp.bfloat16),
             pltpu.VMEM((SWEEPS, nb * rows, LANES), jnp.bfloat16),
             pltpu.VMEM((elems, rows, LANES), jnp.float32),
-            pltpu.SemaphoreType.DMA(()),
+            pltpu.SemaphoreType.DMA((3,)),
             pltpu.SemaphoreType.DMA((SWEEPS, 3, nb)),
             pltpu.SemaphoreType.DMA((SWEEPS, 3, nb)),
             pltpu.SemaphoreType.DMA((SWEEPS, nb)),
@@ -434,8 +450,7 @@
             collective_id=0, has_side_effects=True, vmem_limit_bytes=48 * 1024 * 1024
         ),
     )(
-        transposed(adjoint_start),
-        transposed(right_sides),
+        transposed(jnp.stack([adjoint_start, right_sides])),
         shift,
         target,
         jac_blocks,

time: 73.4 us -> 74 us (level)
    transpose x2 -> x1, local copies, waits for them, and re-layouts: 1.57 us -> 0.04 us  [transposed(): x = jnp.transpose(x, (0, 3, 1, 2)).reshape(x.shape[0], rows, elems * rhs)]
    unnamed x6, local copies, waits for them, and re-layouts: 3.32 us -> 4.51 us
    transpose x0 -> x1, other arithmetic: none -> 0.8 us  [transposed(): x = jnp.transpose(x, (0, 3, 1, 2)).reshape(x.shape[0], rows, elems * rhs)]
where the time goes in v6:
time: 74 us; the launch traced here: 73.7 us
  Pallas kernels  59.8 us (81%)
  local copies, waits for them, and re-layouts  8.35 us (11%)
  other arithmetic  4.78 us (6%)
  between operations  0.76 us (1%)
    pallas_call x1, Pallas kernels, sweeps(): pl.pallas_call(_sweeps_kernel, out_shape=(jax.ShapeDtypeStruct((rows, LAN...  46.2 us
    pallas_call x1, Pallas kernels, _exchange(): pl.pallas_call(kernel, out_shape=jax.ShapeDtypeStruct(out_shape, x.dtype)...  13.5 us
    unnamed x6, local copies, waits for them, and re-layouts  4.51 us
    scatter-add x1, other arithmetic, local(): partial_sums = jax.ops.segment_sum(values, node_slots, 3 * NODE_DEV).T  2.54 us

profile of v6, /device:TPU:7, one launch (start us, length us, event | category | flops | bytes accessed | tf_op | source)
XLA Modules:
  0.0 73.7 jit_solution(1524826267439303464)
XLA Ops:
  0.6 0.7 dynamic-slice_subtract_fusion
  1.4 0.1 reshape.93
  1.4 0.7 broadcast_subtract_fusion
  2.2 0.1 copy.22
  2.2 0.7 broadcast_in_dim.12
  3.0 0.1 reshape.85
  3.1 0.1 add.79
  3.2 0.1 copy.23
  3.3 0.8 %maximum_bitcast_fusion = f32[2,80,24,3]{1,2,3,0:T(8,128)S(1)} fusion(f32[1,24,3,80]{3,1,2,0:T(8,128)} %bitcast.32, f32[1,24,3,80]{3,1,2,0:T(8,128)} %bitcast.33), kind=kLoop, calls=%fused_computation.3 | loop fusion | flops 11520 | bytes 92160 | tf_op jit(solution)/shard_map/transpose | solution.py:410
  4.2 0.1 copy.21
  4.3 0.0 copy-start
  4.3 1.4 %copy-done = bf16[24,80,320]{2,1,0:T(8,128)(2,1)S(1)} copy-done((bf16[24,80,320]{2,1,0:T(8,128)(2,1)S(1)}, bf16[24,80,320]{2,1,0:T(8,128)(2,1)}, u32[]{:S(2)}) %copy-start) | copy-done | bytes 1228824
  5.6 0.0 copy-start.1
  5.7 1.2 %copy-done.1 = bf16[24,80,192]{2,1,0:T(8,128)(2,1)S(1)} copy-done((bf16[24,80,192]{2,1,0:T(8,128)(2,1)S(1)}, bf16[24,80,192]{2,1,0:T(8,128)(2,1)}, u32[]{:S(2)}) %copy-start.1) | copy-done | bytes 737304
  6.9 46.2 %shard_map.95 = (f32[80,128]{1,0:T(8,128)S(1)}, f32[24,192]{1,0:T(8,128)S(1)}) custom-call(f32[2,80,128]{2,1,0:T(8,128)S(1)} %pad.12.start_ref, f32[1,128]{1,0:T(1,128)S(1)} %pad_bitcast_fusion.shift_ref, s32[8,128]{1,0:T(8,128)S(1)} %pad.14.target_ref, bf16[24,7,80,320]{3,2,1,0:T(8,128)(2,1)} %jac_hbm.1, bf16[1920,320]{1,0:T(8,128)(2,1)S(1)} %bitcast.25, ...), custom_call_target="tpu_custom_call" | custom-call | tf_op jit(solution)/shard_map/pallas_call | solution.py:421
  53.1 0.1 copy.24
  53.2 0.6 copy.29
  53.8 0.7 %reshape.88 = f32[8,3,64,3]{3,2,1,0:T(8,128)S(1)} reshape(f32[24,192]{1,0:T(8,128)S(1)} %get-tuple-element.5) | data formatting | bytes 36864 | tf_op jit(solution)/shard_map/reshape | solution.py:485
  54.6 0.3 copy.25
  54.9 0.1 reshape.95
  54.9 0.1 copy.26
  55.1 2.5 %scatter_custom_fusion = f32[2304,9]{1,0:T(8,128)S(1)} fusion(s32[512]{0:T(512)S(1)} %reshape.93, f32[512,9]{1,0:T(8,128)S(1)} %copy.26, f32[]{:T(128)} %constant.15.clone.1), kind=kCustom, calls=%fused_computation.1 | custom fusion | flops 4608 | bytes 82948 | tf_op jit(solution)/shard_map/scatter-add | solution.py:492
  57.6 1.1 %copy.28 = f32[9,3,4,192]{3,0,2,1:T(8,128)} copy(f32[9,3,4,192]{0,3,2,1:T(8,128)S(1)} %bitcast.27) | data formatting | bytes 165888 | tf_op jit(solution)/shard_map/reshape | solution.py:494
  58.8 13.5 %shard_map.96 = f32[9,192]{1,0:T(8,128)} custom-call(f32[3,4,9,192]{3,2,1,0:T(8,128)} %bitcast.29), custom_call_target="tpu_custom_call" | custom-call | tf_op jit(solution)/shard_map/pallas_call | solution.py:158
  72.3 1.3 %copy.33 = f32[9,192]{1,0:T(8,128)} copy(f32[9,192]{1,0:T(8,128)} %shard_map.96) | data formatting | bytes 13824
  (11 shorter events, 0.2 us)
Async XLA Ops:
  4.3 1.4 %copy-start = (bf16[24,80,320]{2,1,0:T(8,128)(2,1)S(1)}, bf16[24,80,320]{2,1,0:T(8,128)(2,1)}, u32[]{:S(2)}) copy-start(bf16[24,80,320]{2,1,0:T(8,128)(2,1)} %param.11) | copy-start | bytes 3686404
  5.6 1.2 %copy-start.1 = (bf16[24,80,192]{2,1,0:T(8,128)(2,1)S(1)}, bf16[24,80,192]{2,1,0:T(8,128)(2,1)}, u32[]{:S(2)}) copy-start(bf16[24,80,192]{2,1,0:T(8,128)(2,1)} %shape_hbm.1) | copy-start | bytes 2211844

commit v7 on v6

--- a/solution.py
+++ b/solution.py
@@ -196,7 +196,7 @@
 
 
 def _sweeps_kernel(
-    start_ref, shift_ref, target_ref, jac_hbm, inv_hbm, shape_hbm, out_ref, wsum_ref,
+    start_ref, shift_ref, slot_ref, jac_hbm, inv_hbm, shape_hbm, out_ref, wsum_ref,
     jac_v, inv_ref, shape_ref, select, send_a, halo, send_r, full_r, upd, jac_sem, hs_send, hs_recv, bk_send, bk_recv,
     fw_send, wpart, ws_send, ws_recv,
 ):
@@ -218,9 +218,21 @@
     inv_copy.start()
     shape_copy.start()
     lane = lax.broadcasted_iota(jnp.int32, (rows, LANES), 1)
+    sub = lax.broadcasted_iota(jnp.int32, (8, LANES), 0)
+    lane8 = lax.broadcasted_iota(jnp.int32, (8, LANES), 1)
+    target = jnp.full((8, LANES), -1, jnp.int32)
+    shift = jnp.zeros((8, LANES), jnp.float32)
+    for e in range(elems):
+        mine = lane8 // RHS == e
+        shift = jnp.where(mine, shift_ref[e], shift)
+        for k in range(faces):
+            slot = elems + e if k == 0 else slot_ref[e, k - 1] - (d - 1) * elems
+            base = slot // elems * LANES + slot % elems * RHS
+            target = jnp.where(mine & (sub == k), base + lane8 % RHS, target)
+    shift = shift[0:1]
     cand_row = lax.broadcasted_iota(jnp.int32, (3 * LANES, LANES), 0)
     for k in range(faces):
-        select[k] = (cand_row == target_ref[pl.ds(k, 1), :]).astype(jnp.bfloat16)
+        select[k] = (cand_row == target[k:k + 1]).astype(jnp.bfloat16)
 
     def row_block(i):
         return pl.ds(pl.multiple_of(i * rows, 16), rows)
@@ -305,7 +317,7 @@
         for e in range(elems):
             mine = (lane >= RHS * e) & (lane < RHS * e + RHS)
             product = product + jnp.where(mine, upd[e], 0.0)
-        image = shift_ref[...] * adjoint + product
+        image = shift * adjoint + product
         send_r[sweep] = (start_ref[1] - image).astype(jnp.bfloat16)
 
         def blk_copy(m, sweep=sweep):
@@ -400,7 +412,7 @@
         wsum_ref[...] = jnp.zeros(wsum_ref.shape, jnp.float32)
 
 
-def sweeps(adjoint_start, right_sides, pseudo_shift, slots, jac_blocks, block_inverse,
+def sweeps(adjoint_start, right_sides, pseudo_shift, neighbours, jac_blocks, block_inverse,
            shape_partials, nb):
     elems, rhs, rows = adjoint_start.shape
     cols = jac_blocks.shape[-1]
@@ -410,13 +422,9 @@
         x = jnp.transpose(x, (0, 3, 1, 2)).reshape(x.shape[0], rows, elems * rhs)
         return jnp.pad(x, ((0, 0), (0, 0), (0, LANES - elems * rhs)))
 
-    shift = jnp.pad(jnp.repeat(pseudo_shift, rhs), (0, LANES - elems * rhs))[None, :]
-    part, within = slots // elems, slots % elems
-    lanes = (part * LANES + within * rhs)[:, :, None] + jnp.arange(rhs, dtype=jnp.int32)
-    target = jnp.transpose(lanes, (1, 0, 2)).reshape(faces, elems * rhs)
-    target = jnp.pad(target, ((0, 8 - faces), (0, LANES - elems * rhs)), constant_values=-1)
     vmem = pl.BlockSpec(memory_space=pltpu.VMEM)
     hbm = pl.BlockSpec(memory_space=pl.ANY)
+    smem = pl.BlockSpec(memory_space=pltpu.SMEM)
     chunk = 8 * rhs
     out, wsum = pl.pallas_call(
         _sweeps_kernel,
@@ -424,7 +432,7 @@
             jax.ShapeDtypeStruct((rows, LANES), jnp.float32),
             jax.ShapeDtypeStruct((chunk, shape_partials.shape[2]), jnp.float32),
         ),
-        in_specs=[vmem, vmem, vmem, hbm, hbm, hbm],
+        in_specs=[vmem, smem, smem, hbm, hbm, hbm],
         out_specs=(vmem, vmem),
         scratch_shapes=[
             pltpu.VMEM((elems, faces, rows, cols), jnp.bfloat16),
@@ -447,12 +455,12 @@
             pltpu.SemaphoreType.DMA((nb,)),
         ],
         compiler_params=pltpu.CompilerParams(
-            collective_id=0, has_side_effects=True, vmem_limit_bytes=48 * 1024 * 1024
+            collective_id=0, has_side_effects=True, vmem_limit_bytes=67043328
         ),
     )(
         transposed(jnp.stack([adjoint_start, right_sides])),
-        shift,
-        target,
+        pseudo_shift,
+        neighbours,
         jac_blocks,
         block_inverse.reshape(elems * rows, cols),
         shape_partials,
@@ -474,10 +482,8 @@
     local_count = neighbours.shape[0]
     nb = lax.axis_size("blk")
     part_index = lax.axis_index("dom")
-    own = jnp.arange(local_count, dtype=jnp.int32)[:, None] + local_count
-    slots = jnp.concatenate([own, neighbours - (part_index - 1) * local_count], axis=1)
     adjoint, wsum = sweeps(
-        adjoint_start, right_sides, pseudo_shift, slots, jac_blocks, block_inverse,
+        adjoint_start, right_sides, pseudo_shift, neighbours, jac_blocks, block_inverse,
         shape_partials, nb,
     )
     node_width = node_ids.shape[1]

time: 74 us -> 75.9 us (1.026)
  Pallas kernels: 59.8 us -> 61.9 us
    pallas_call x1, Pallas kernels: 46.2 us -> 48.3 us  [sweeps(): pl.pallas_call(_sweeps_kernel, out_shape=(jax.ShapeDtypeStruct((rows, LAN...]
    unnamed x6 -> x3, local copies, waits for them, and re-layouts: 4.51 us -> 3.31 us
    slice x1, local copies, waits for them, and re-layouts: 0.07 us -> 0.85 us  [sweeps(): out[:, :elems * rhs].reshape(rows, elems, rhs)]
where the time goes in v7:
time: 75.9 us; the launch traced here: 75.4 us
  Pallas kernels  61.9 us (82%)
  local copies, waits for them, and re-layouts  8.72 us (11%)
  other arithmetic  4.17 us (5%)
    pallas_call x1, Pallas kernels, sweeps(): pl.pallas_call(_sweeps_kernel, out_shape=(jax.ShapeDtypeStruct((rows, LAN...  48.3 us
    pallas_call x1, Pallas kernels, _exchange(): pl.pallas_call(kernel, out_shape=jax.ShapeDtypeStruct(out_shape, x.dtype)...  13.5 us
    unnamed x3, local copies, waits for them, and re-layouts  3.31 us
    scatter-add x1, other arithmetic, local(): partial_sums = jax.ops.segment_sum(values, node_slots, 3 * NODE_DEV).T  2.66 us

profile of v7, /device:TPU:7, one launch (start us, length us, event | category | flops | bytes accessed | tf_op | source)
XLA Modules:
  0.0 75.4 jit_solution(7498075073555767275)
XLA Ops:
  0.6 0.7 dynamic-slice_subtract_fusion
  1.3 0.6 reshape.30
  2.0 1.4 %copy.22.slot_ref = s32[24,6]{1,0:T(8,128)} copy(s32[24,6]{0,1:T(8,128)} %param.12) | data formatting | bytes 1152 | tf_op args[4]
  3.4 0.8 %maximum_bitcast_fusion = f32[2,80,24,3]{1,2,3,0:T(8,128)S(1)} fusion(f32[1,24,3,80]{3,1,2,0:T(8,128)} %bitcast.26, f32[1,24,3,80]{3,1,2,0:T(8,128)} %bitcast.27), kind=kLoop, calls=%fused_computation.3 | loop fusion | flops 11520 | bytes 92160 | tf_op jit(solution)/shard_map/transpose | solution.py:422
  4.2 0.1 copy.21
  4.3 0.6 pad.4.start_ref
  4.9 48.3 %shard_map.95 = (f32[80,128]{1,0:T(8,128)}, f32[24,192]{1,0:T(8,128)}) custom-call(f32[2,80,128]{2,1,0:T(8,128)} %pad.4.start_ref, f32[24]{0:T(128)} %shift_ref.1, s32[24,6]{1,0:T(8,128)} %copy.22.slot_ref, bf16[24,7,80,320]{3,2,1,0:T(8,128)(2,1)} %jac_hbm.1, bf16[1920,320]{1,0:T(8,128)(2,1)} %bitcast.21, bf16[24,80,192]{2,1,0:T(8,128)(2,1)} %shape_hbm.1), custom_call_target="tpu_custom_call" | custom-call | tf_op jit(solution)/shard_map/pallas_call | solution.py:429
  53.2 0.9 %copy.23 = f32[80,72]{0,1:T(8,128)S(1)} copy(f32[80,72]{1,0:T(8,128)} %bitcast.25) | data formatting | bytes 46080 | tf_op jit(solution)/shard_map/slice | solution.py:468
  54.1 0.6 copy.28
  54.7 1.5 %reshape.25 = f32[8,3,64,3]{3,2,1,0:T(8,128)S(1)} reshape(f32[24,192]{1,0:T(8,128)} %get-tuple-element.5) | data formatting | bytes 36864 | tf_op jit(solution)/shard_map/reshape | solution.py:491
  56.2 0.3 copy.24
  56.5 0.1 reshape.32
  56.6 0.1 copy.25
  56.8 2.7 %scatter_custom_fusion = f32[2304,9]{1,0:T(8,128)S(1)} fusion(s32[512]{0:T(512)} %reshape.30, f32[512,9]{1,0:T(8,128)S(1)} %copy.25, f32[]{:T(128)} %constant.5.clone.1), kind=kCustom, calls=%fused_computation.1 | custom fusion | flops 4608 | bytes 83456 | tf_op jit(solution)/shard_map/scatter-add | solution.py:498
  59.4 1.1 %copy.27 = f32[9,3,4,192]{3,0,2,1:T(8,128)} copy(f32[9,3,4,192]{0,3,2,1:T(8,128)S(1)} %bitcast.19) | data formatting | bytes 165888 | tf_op jit(solution)/shard_map/reshape | solution.py:500
  60.6 13.5 %shard_map.96 = f32[9,192]{1,0:T(8,128)} custom-call(f32[3,4,9,192]{3,2,1,0:T(8,128)} %bitcast.22), custom_call_target="tpu_custom_call" | custom-call | tf_op jit(solution)/shard_map/pallas_call | solution.py:158
  74.1 1.3 %copy.32 = f32[9,192]{1,0:T(8,128)} copy(f32[9,192]{1,0:T(8,128)} %shard_map.96) | data formatting | bytes 13824
  (2 shorter events, 0.1 us)

commit v8 on v6

--- a/solution.py
+++ b/solution.py
@@ -447,7 +447,7 @@
             pltpu.SemaphoreType.DMA((nb,)),
         ],
         compiler_params=pltpu.CompilerParams(
-            collective_id=0, has_side_effects=True, vmem_limit_bytes=48 * 1024 * 1024
+            collective_id=0, has_side_effects=True, vmem_limit_bytes=67043328
         ),
     )(
         transposed(jnp.stack([adjoint_start, right_sides])),

time: 74 us -> 76.4 us (1.032)
  local copies, waits for them, and re-layouts: 8.35 us -> 9.59 us
  Pallas kernels: 59.8 us -> 60.7 us
    unnamed x6 -> x2, local copies, waits for them, and re-layouts: 4.51 us -> 1.94 us
    pallas_call x1, Pallas kernels: 46.2 us -> 47.1 us  [sweeps(): pl.pallas_call(_sweeps_kernel, out_shape=(jax.ShapeDtypeStruct((rows, LAN...]
    slice x1, local copies, waits for them, and re-layouts: 0.07 us -> 0.85 us  [sweeps(): out[:, :elems * rhs].reshape(rows, elems, rhs)]
where the time goes in v8:
time: 76.4 us; the launch traced here: 75.9 us
  Pallas kernels  60.7 us (79%)
  local copies, waits for them, and re-layouts  9.59 us (13%)
  other arithmetic  4.89 us (6%)
    pallas_call x1, Pallas kernels, sweeps(): pl.pallas_call(_sweeps_kernel, out_shape=(jax.ShapeDtypeStruct((rows, LAN...  47.1 us
    pallas_call x1, Pallas kernels, _exchange(): pl.pallas_call(kernel, out_shape=jax.ShapeDtypeStruct(out_shape, x.dtype)...  13.5 us
    scatter-add x1, other arithmetic, local(): partial_sums = jax.ops.segment_sum(values, node_slots, 3 * NODE_DEV).T  2.66 us
    unnamed x2, local copies, waits for them, and re-layouts  1.94 us

profile of v8, /device:TPU:7, one launch (start us, length us, event | category | flops | bytes accessed | tf_op | source)
XLA Modules:
  0.0 75.9 jit_solution(4308411028733663915)
XLA Ops:
  0.6 0.7 dynamic-slice_subtract_fusion
  1.4 0.6 reshape.93
  2.0 0.7 broadcast_subtract_fusion
  2.7 0.1 copy.22
  2.8 0.7 broadcast_in_dim.12
  3.5 0.1 reshape.85
  3.6 0.5 pad_bitcast_fusion.shift_ref
  4.1 0.1 add.79
  4.3 0.1 copy.23
  4.4 0.6 pad.14.target_ref
  5.0 0.8 %maximum_bitcast_fusion = f32[2,80,24,3]{1,2,3,0:T(8,128)S(1)} fusion(f32[1,24,3,80]{3,1,2,0:T(8,128)} %bitcast.32, f32[1,24,3,80]{3,1,2,0:T(8,128)} %bitcast.33), kind=kLoop, calls=%fused_computation.3 | loop fusion | flops 11520 | bytes 92160 | tf_op jit(solution)/shard_map/transpose | solution.py:410
  5.8 0.1 copy.21
  5.9 0.6 pad.12.start_ref
  6.5 47.1 %shard_map.95 = (f32[80,128]{1,0:T(8,128)}, f32[24,192]{1,0:T(8,128)}) custom-call(f32[2,80,128]{2,1,0:T(8,128)} %pad.12.start_ref, f32[1,128]{1,0:T(1,128)} %pad_bitcast_fusion.shift_ref, s32[8,128]{1,0:T(8,128)} %pad.14.target_ref, bf16[24,7,80,320]{3,2,1,0:T(8,128)(2,1)} %jac_hbm.1, bf16[1920,320]{1,0:T(8,128)(2,1)} %bitcast.27, ...), custom_call_target="tpu_custom_call" | custom-call | tf_op jit(solution)/shard_map/pallas_call | solution.py:421
  53.7 0.9 %copy.24 = f32[80,72]{0,1:T(8,128)S(1)} copy(f32[80,72]{1,0:T(8,128)} %bitcast.31) | data formatting | bytes 46080 | tf_op jit(solution)/shard_map/slice | solution.py:460
  54.6 0.6 copy.29
  55.2 1.5 %reshape.88 = f32[8,3,64,3]{3,2,1,0:T(8,128)S(1)} reshape(f32[24,192]{1,0:T(8,128)} %get-tuple-element.5) | data formatting | bytes 36864 | tf_op jit(solution)/shard_map/reshape | solution.py:485
  56.7 0.3 copy.25
  57.0 0.1 reshape.95
  57.1 0.1 copy.26
  57.2 2.7 %scatter_custom_fusion = f32[2304,9]{1,0:T(8,128)S(1)} fusion(s32[512]{0:T(512)} %reshape.93, f32[512,9]{1,0:T(8,128)S(1)} %copy.26, f32[]{:T(128)} %constant.15.clone.1), kind=kCustom, calls=%fused_computation.1 | custom fusion | flops 4608 | bytes 83456 | tf_op jit(solution)/shard_map/scatter-add | solution.py:492
  59.9 1.1 %copy.28 = f32[9,3,4,192]{3,0,2,1:T(8,128)} copy(f32[9,3,4,192]{0,3,2,1:T(8,128)S(1)} %bitcast.25) | data formatting | bytes 165888 | tf_op jit(solution)/shard_map/reshape | solution.py:494
  61.0 13.5 %shard_map.96 = f32[9,192]{1,0:T(8,128)} custom-call(f32[3,4,9,192]{3,2,1,0:T(8,128)} %bitcast.28), custom_call_target="tpu_custom_call" | custom-call | tf_op jit(solution)/shard_map/pallas_call | solution.py:158
  74.6 1.3 %copy.33 = f32[9,192]{1,0:T(8,128)} copy(f32[9,192]{1,0:T(8,128)} %shard_map.96) | data formatting | bytes 13824
  (8 shorter events, 0.1 us)

commit v9 on v5

--- a/solution.py
+++ b/solution.py
@@ -196,13 +196,13 @@
 
 
 def _sweeps_kernel(
-    adj_ref, rs_ref, shift_ref, target_ref, jac_hbm, inv_ref, shape_ref, out_ref, wsum_ref,
+    start_ref, target_ref, jac_hbm, inv_ref, shape_ref, out_ref, wsum_ref,
     jac_v, select, send_a, halo, send_r, full_r, upd, jac_sem, hs_send, hs_recv, bk_send, bk_recv,
     fw_send, wpart, ws_send, ws_recv,
 ):
     d, b = lax.axis_index("dom"), lax.axis_index("blk")
     nd, nb = lax.axis_size("dom"), lax.axis_size("blk")
-    rows = adj_ref.shape[0]
+    rows = start_ref.shape[1]
     elems = jac_v.shape[0]
     faces = jac_v.shape[1]
 
@@ -222,7 +222,7 @@
         return pl.ds(pl.multiple_of(i * rows, 16), rows)
 
     own_rows = row_block(b)
-    adjoint = adj_ref[...]
+    adjoint = start_ref[0]
     for sweep in range(SWEEPS):
         send_a[sweep] = adjoint.astype(jnp.bfloat16)
 
@@ -301,8 +301,8 @@
         for e in range(elems):
             mine = (lane >= RHS * e) & (lane < RHS * e + RHS)
             product = product + jnp.where(mine, upd[e], 0.0)
-        image = shift_ref[...] * adjoint + product
-        send_r[sweep] = (rs_ref[...] - image).astype(jnp.bfloat16)
+        image = start_ref[2] * adjoint + product
+        send_r[sweep] = (start_ref[1] - image).astype(jnp.bfloat16)
 
         def blk_copy(m, sweep=sweep):
             return pltpu.make_async_remote_copy(
@@ -393,11 +393,13 @@
     cols = jac_blocks.shape[-1]
     faces = jac_blocks.shape[1]
 
-    def transposed(x):
-        x = jnp.transpose(x, (2, 0, 1)).reshape(rows, elems * rhs)
-        return jnp.pad(x, ((0, 0), (0, LANES - elems * rhs)))
-
-    shift = jnp.pad(jnp.repeat(pseudo_shift, rhs), (0, LANES - elems * rhs))[None, :]
+    stacked = jnp.stack([
+        adjoint_start,
+        right_sides,
+        jnp.broadcast_to(pseudo_shift[:, None, None], adjoint_start.shape),
+    ])
+    stacked = jnp.transpose(stacked, (0, 3, 1, 2)).reshape(3, rows, elems * rhs)
+    stacked = jnp.pad(stacked, ((0, 0), (0, 0), (0, LANES - elems * rhs)))
     part, within = slots // elems, slots % elems
     lanes = (part * LANES + within * rhs)[:, :, None] + jnp.arange(rhs, dtype=jnp.int32)
     target = jnp.transpose(lanes, (1, 0, 2)).reshape(faces, elems * rhs)
@@ -410,7 +412,7 @@
             jax.ShapeDtypeStruct((rows, LANES), jnp.float32),
             jax.ShapeDtypeStruct((chunk, shape_partials.shape[2]), jnp.float32),
         ),
-        in_specs=[vmem, vmem, vmem, vmem, pl.BlockSpec(memory_space=pl.ANY), vmem, vmem],
+        in_specs=[vmem, vmem, pl.BlockSpec(memory_space=pl.ANY), vmem, vmem],
         out_specs=(vmem, vmem),
         scratch_shapes=[
             pltpu.VMEM((elems, faces, rows, cols), jnp.bfloat16),
@@ -434,9 +436,7 @@
             collective_id=0, has_side_effects=True, vmem_limit_bytes=48 * 1024 * 1024
         ),
     )(
-        transposed(adjoint_start),
-        transposed(right_sides),
-        shift,
+        stacked,
         target,
         jac_blocks,
         block_inverse.reshape(elems * rows, cols),

time: 73.4 us -> 72.3 us (0.985)
  local copies, waits for them, and re-layouts: 8.8 us -> 6.97 us
  other arithmetic: 4.06 us -> 4.88 us
    transpose x2 -> x1, local copies, waits for them, and re-layouts: 1.57 us -> 0.04 us  [sweeps(): stacked = jnp.transpose(stacked, (0, 3, 1, 2)).reshape(3, rows, elems * rhs)]
    transpose x0 -> x1, other arithmetic: none -> 0.8 us  [sweeps(): stacked = jnp.transpose(stacked, (0, 3, 1, 2)).reshape(3, rows, elems * rhs)]
where the time goes in v9:
time: 72.3 us; the launch traced here: 72 us
  Pallas kernels  59.4 us (82%)
  local copies, waits for them, and re-layouts  6.97 us (10%)
  other arithmetic  4.88 us (7%)
  between operations  0.77 us (1%)
    pallas_call x1, Pallas kernels, sweeps(): pl.pallas_call(_sweeps_kernel, out_shape=(jax.ShapeDtypeStruct((rows, LAN...  45.8 us
    pallas_call x1, Pallas kernels, _exchange(): pl.pallas_call(kernel, out_shape=jax.ShapeDtypeStruct(out_shape, x.dtype)...  13.5 us
    unnamed x6, local copies, waits for them, and re-layouts  3.15 us
    scatter-add x1, other arithmetic, local(): partial_sums = jax.ops.segment_sum(values, node_slots, 3 * NODE_DEV).T  2.54 us

profile of v9, /device:TPU:7, one launch (start us, length us, event | category | flops | bytes accessed | tf_op | source)
XLA Modules:
  0.0 72.0 jit_solution(10691106094575888289)
XLA Ops:
  0.6 0.0 copy-start
  0.7 0.8 %dynamic-slice_subtract_fusion = s32[8,64]{1,0:T(8,128)S(1)} fusion(s32[24,64]{1,0:T(8,128)} %param.15, s32[]{:T(128)S(6)} %select_n.25, s32[]{:T(128)S(6)} %mul.35), kind=kLoop, calls=%fused_computation.11 | loop fusion | flops 512 | bytes 4104 | tf_op jit(solution)/shard_map/sub | solution.py:476
  1.5 0.1 reshape.94
  1.6 0.7 broadcast_subtract_fusion
  2.3 0.1 copy.22
  2.4 0.1 add.77
  2.5 0.1 copy.23
  2.6 0.7 %stack_broadcast_in_dim.2 = f32[1,24,3,80]{3,1,2,0:T(8,128)S(1)} broadcast(f32[24]{0:T(128)} %param.13), dimensions={1} | broadcast | bytes 23136 | tf_op jit(solution)/shard_map/stack;broadcast_in_dim | solution.py:396
  3.3 0.8 %maximum_bitcast_fusion = f32[3,80,24,3]{1,2,3,0:T(8,128)S(1)} fusion(f32[1,24,3,80]{3,1,2,0:T(8,128)S(1)} %stack_broadcast_in_dim.2, f32[1,24,3,80]{3,1,2,0:T(8,128)} %bitcast.30, f32[1,24,3,80]{3,1,2,0:T(8,128)} %bitcast.31), kind=kLoop, calls=%fused_computation.3 | loop fusion | flops 34560 | bytes 138240 | tf_op jit(solution)/shard_map/transpose | solution.py:401
  4.2 0.1 reshape.86
  4.2 0.1 copy.21
  4.4 0.0 copy-done
  4.4 0.0 copy-start.1
  4.4 1.2 %copy-done.1 = bf16[24,80,192]{2,1,0:T(8,128)(2,1)S(1)} copy-done((bf16[24,80,192]{2,1,0:T(8,128)(2,1)S(1)}, bf16[24,80,192]{2,1,0:T(8,128)(2,1)}, u32[]{:S(2)}) %copy-start.1) | copy-done | bytes 737304
  5.6 45.8 %shard_map.95 = (f32[80,128]{1,0:T(8,128)S(1)}, f32[24,192]{1,0:T(8,128)S(1)}) custom-call(f32[3,80,128]{2,1,0:T(8,128)S(1)} %pad.8.start_ref, s32[8,128]{1,0:T(8,128)S(1)} %pad.9.target_ref, bf16[24,7,80,320]{3,2,1,0:T(8,128)(2,1)} %jac_hbm.1, bf16[1920,320]{1,0:T(8,128)(2,1)S(1)} %bitcast.24, bf16[24,80,192]{2,1,0:T(8,128)(2,1)S(1)} %copy-done.1), custom_call_target="tpu_custom_call" | custom-call | tf_op jit(solution)/shard_map/pallas_call | solution.py:409
  51.4 0.1 copy.24
  51.5 0.6 copy.29
  52.2 0.7 %reshape.89 = f32[8,3,64,3]{3,2,1,0:T(8,128)S(1)} reshape(f32[24,192]{1,0:T(8,128)S(1)} %get-tuple-element.5) | data formatting | bytes 36864 | tf_op jit(solution)/shard_map/reshape | solution.py:470
  52.9 0.3 copy.25
  53.2 0.1 reshape.96
  53.3 0.1 copy.26
  53.4 2.5 %scatter_custom_fusion = f32[2304,9]{1,0:T(8,128)S(1)} fusion(s32[512]{0:T(512)S(1)} %reshape.94, f32[512,9]{1,0:T(8,128)S(1)} %copy.26, f32[]{:T(128)} %constant.15.clone.1), kind=kCustom, calls=%fused_computation.1 | custom fusion | flops 4608 | bytes 82948 | tf_op jit(solution)/shard_map/scatter-add | solution.py:477
  56.0 1.1 %copy.28 = f32[9,3,4,192]{3,0,2,1:T(8,128)} copy(f32[9,3,4,192]{0,3,2,1:T(8,128)S(1)} %bitcast.26) | data formatting | bytes 165888 | tf_op jit(solution)/shard_map/reshape | solution.py:479
  57.1 13.5 %shard_map.96 = f32[9,192]{1,0:T(8,128)} custom-call(f32[3,4,9,192]{3,2,1,0:T(8,128)} %bitcast.28), custom_call_target="tpu_custom_call" | custom-call | tf_op jit(solution)/shard_map/pallas_call | solution.py:158
  70.7 1.3 %copy.33 = f32[9,192]{1,0:T(8,128)} copy(f32[9,192]{1,0:T(8,128)} %shard_map.96) | data formatting | bytes 13824
  (10 shorter events, 0.2 us)
Async XLA Ops:
  0.6 3.7 %copy-start = (bf16[24,80,320]{2,1,0:T(8,128)(2,1)S(1)}, bf16[24,80,320]{2,1,0:T(8,128)(2,1)}, u32[]{:S(2)}) copy-start(bf16[24,80,320]{2,1,0:T(8,128)(2,1)} %param.11) | copy-start | bytes 3686404
  4.4 1.2 %copy-start.1 = (bf16[24,80,192]{2,1,0:T(8,128)(2,1)S(1)}, bf16[24,80,192]{2,1,0:T(8,128)(2,1)}, u32[]{:S(2)}) copy-start(bf16[24,80,192]{2,1,0:T(8,128)(2,1)} %shape_ref.1) | copy-start | bytes 2211844

commit v10 on v9

--- a/solution.py
+++ b/solution.py
@@ -135,7 +135,11 @@
 
     for delta, m in partners:
         pl.when(in_range(d + delta))(lambda delta=delta, m=m: outgoing(delta, m).start())
-    out_ref[...] = x_ref[1, b]
+    buf[1, b] = x_ref[1, b]
+    for side in (-1, 1):
+        @pl.when(jnp.logical_not(in_range(d + side)))
+        def _(side=side):
+            buf[1 - side] = jnp.zeros(buf.shape[1:], buf.dtype)
     for delta, m in partners:
         pl.when(in_range(d + delta))(lambda delta=delta, m=m: outgoing(delta, m).wait_send())
     for delta, m in partners:
@@ -151,7 +155,7 @@
                 device_id=(d - delta, s),
                 device_id_type=MESH,
             ).wait_recv()
-            out_ref[...] += buf[p, s]
+    out_ref[...] = buf[...]
 
 
 def _exchange(kernel, x, out_shape, buf_shape, sem_shape, collective_id):
@@ -187,9 +191,10 @@
 
 def node_reduce(chunks, collective_id):
     nb = chunks.shape[1]
-    return _exchange(
-        _node_reduce_kernel, chunks, chunks.shape[2:], chunks.shape, (3, nb), collective_id
+    received = _exchange(
+        _node_reduce_kernel, chunks, chunks.shape, chunks.shape, (3, nb), collective_id
     )
+    return jnp.sum(received, axis=(0, 1))
 
 
 LANES = 128

time: 72.3 us -> 72.6 us (level)
  other arithmetic: 4.88 us -> 6.44 us
  local copies, waits for them, and re-layouts: 6.97 us -> 5.64 us
    reduce_sum x0 -> x1, other arithmetic: none -> 1.55 us  [node_reduce(): return jnp.sum(received, axis=(0, 1))]
    unnamed x6 -> x5, local copies, waits for them, and re-layouts: 3.15 us -> 1.82 us
where the time goes in v10:
time: 72.6 us; the launch traced here: 72.3 us
  Pallas kernels  59.5 us (82%)
  other arithmetic  6.44 us (9%)
  local copies, waits for them, and re-layouts  5.64 us (8%)
  between operations  0.77 us (1%)
    pallas_call x1, Pallas kernels, sweeps(): pl.pallas_call(_sweeps_kernel, out_shape=(jax.ShapeDtypeStruct((rows, LAN...  45.8 us
    pallas_call x1, Pallas kernels, _exchange(): pl.pallas_call(kernel, out_shape=jax.ShapeDtypeStruct(out_shape, x.dtype)...  13.6 us
    scatter-add x1, other arithmetic, local(): partial_sums = jax.ops.segment_sum(values, node_slots, 3 * NODE_DEV).T  2.54 us
    unnamed x5, local copies, waits for them, and re-layouts  1.82 us
    reduce_sum x1, other arithmetic, node_reduce(): return jnp.sum(received, axis=(0, 1))  1.55 us

profile of v10, /device:TPU:7, one launch (start us, length us, event | category | flops | bytes accessed | tf_op | source)
XLA Modules:
  0.0 72.3 jit_solution(13589358077590782149)
XLA Ops:
  0.6 0.0 copy-start
  0.7 0.8 %dynamic-slice_subtract_fusion = s32[8,64]{1,0:T(8,128)S(1)} fusion(s32[24,64]{1,0:T(8,128)} %param.15, s32[]{:T(128)S(6)} %select_n.25, s32[]{:T(128)S(6)} %mul.35), kind=kLoop, calls=%fused_computation.11 | loop fusion | flops 512 | bytes 4104 | tf_op jit(solution)/shard_map/sub | solution.py:481
  1.5 0.1 reshape.94
  1.6 0.7 broadcast_subtract_fusion
  2.3 0.1 copy.22
  2.4 0.1 add.77
  2.5 0.1 copy.23
  2.6 0.7 %stack_broadcast_in_dim.2 = f32[1,24,3,80]{3,1,2,0:T(8,128)S(1)} broadcast(f32[24]{0:T(128)} %param.13), dimensions={1} | broadcast | bytes 23136 | tf_op jit(solution)/shard_map/stack;broadcast_in_dim | solution.py:401
  3.3 0.8 %maximum_bitcast_fusion = f32[3,80,24,3]{1,2,3,0:T(8,128)S(1)} fusion(f32[1,24,3,80]{3,1,2,0:T(8,128)S(1)} %stack_broadcast_in_dim.2, f32[1,24,3,80]{3,1,2,0:T(8,128)} %bitcast.30, f32[1,24,3,80]{3,1,2,0:T(8,128)} %bitcast.31), kind=kLoop, calls=%fused_computation.3 | loop fusion | flops 34560 | bytes 138240 | tf_op jit(solution)/shard_map/transpose | solution.py:406
  4.2 0.1 reshape.86
  4.2 0.1 copy.21
  4.4 0.0 copy-done
  4.4 0.0 copy-start.1
  4.4 1.2 %copy-done.1 = bf16[24,80,192]{2,1,0:T(8,128)(2,1)S(1)} copy-done((bf16[24,80,192]{2,1,0:T(8,128)(2,1)S(1)}, bf16[24,80,192]{2,1,0:T(8,128)(2,1)}, u32[]{:S(2)}) %copy-start.1) | copy-done | bytes 737304
  5.6 45.8 %shard_map.95 = (f32[80,128]{1,0:T(8,128)S(1)}, f32[24,192]{1,0:T(8,128)S(1)}) custom-call(f32[3,80,128]{2,1,0:T(8,128)S(1)} %pad.8.start_ref, s32[8,128]{1,0:T(8,128)S(1)} %pad.9.target_ref, bf16[24,7,80,320]{3,2,1,0:T(8,128)(2,1)} %jac_hbm.1, bf16[1920,320]{1,0:T(8,128)(2,1)S(1)} %bitcast.24, bf16[24,80,192]{2,1,0:T(8,128)(2,1)S(1)} %copy-done.1), custom_call_target="tpu_custom_call" | custom-call | tf_op jit(solution)/shard_map/pallas_call | solution.py:414
  51.4 0.1 copy.24
  51.5 0.6 copy.29
  52.2 0.7 %reshape.89 = f32[8,3,64,3]{3,2,1,0:T(8,128)S(1)} reshape(f32[24,192]{1,0:T(8,128)S(1)} %get-tuple-element.5) | data formatting | bytes 36864 | tf_op jit(solution)/shard_map/reshape | solution.py:475
  52.9 0.3 copy.25
  53.2 0.1 reshape.96
  53.3 0.1 copy.26
  53.4 2.5 %scatter_custom_fusion = f32[2304,9]{1,0:T(8,128)S(1)} fusion(s32[512]{0:T(512)S(1)} %reshape.94, f32[512,9]{1,0:T(8,128)S(1)} %copy.26, f32[]{:T(128)} %constant.15.clone.1), kind=kCustom, calls=%fused_computation.1 | custom fusion | flops 4608 | bytes 82948 | tf_op jit(solution)/shard_map/scatter-add | solution.py:482
  56.0 1.1 %copy.28 = f32[9,3,4,192]{3,0,2,1:T(8,128)} copy(f32[9,3,4,192]{0,3,2,1:T(8,128)S(1)} %bitcast.26) | data formatting | bytes 165888 | tf_op jit(solution)/shard_map/reshape | solution.py:484
  57.1 13.6 %shard_map.96 = f32[3,4,9,192]{3,2,1,0:T(8,128)} custom-call(f32[3,4,9,192]{3,2,1,0:T(8,128)} %bitcast.28), custom_call_target="tpu_custom_call" | custom-call | tf_op jit(solution)/shard_map/pallas_call | solution.py:162
  70.8 1.6 %reduce_sum.9 = f32[9,192]{1,0:T(8,128)} reduce(f32[3,4,9,192]{3,2,1,0:T(8,128)} %shard_map.96, f32[]{:T(128)} %constant.15.clone.1), dimensions={0,1}, to_apply=%region_1.2 | reduce | flops 19008 | bytes 89860 | tf_op jit(solution)/shard_map/reduce_sum | solution.py:197
  (10 shorter events, 0.2 us)
Async XLA Ops:
  0.6 3.7 %copy-start = (bf16[24,80,320]{2,1,0:T(8,128)(2,1)S(1)}, bf16[24,80,320]{2,1,0:T(8,128)(2,1)}, u32[]{:S(2)}) copy-start(bf16[24,80,320]{2,1,0:T(8,128)(2,1)} %param.11) | copy-start | bytes 3686404
  4.4 1.2 %copy-start.1 = (bf16[24,80,192]{2,1,0:T(8,128)(2,1)S(1)}, bf16[24,80,192]{2,1,0:T(8,128)(2,1)}, u32[]{:S(2)}) copy-start(bf16[24,80,192]{2,1,0:T(8,128)(2,1)} %shape_ref.1) | copy-start | bytes 2211844

commit v11 on v9

--- a/solution.py
+++ b/solution.py
@@ -210,9 +210,9 @@
         return (i >= 0) & (i < nd)
 
     partners = [(0, m) for m in range(1, nb)] + [(-1, 0), (1, 0)]
-    _barrier(partners, in_range, d, b, nb)
     jac_copy = pltpu.make_async_copy(jac_hbm, jac_v, jac_sem)
     jac_copy.start()
+    _barrier(partners, in_range, d, b, nb)
     lane = lax.broadcasted_iota(jnp.int32, (rows, LANES), 1)
     cand_row = lax.broadcasted_iota(jnp.int32, (3 * LANES, LANES), 0)
     for k in range(faces):
@@ -340,13 +340,19 @@
     out_ref[...] = adjoint
 
     square = jnp.concatenate([adjoint, jnp.zeros((LANES - rows, LANES), jnp.float32)], axis=0)
-    final_half = jnp.transpose(square)[:, :rows].astype(jnp.bfloat16)
-    row = lax.broadcasted_iota(jnp.int32, (LANES, shape_ref.shape[2]), 0)
-    weighted = jnp.zeros((LANES, shape_ref.shape[2]), jnp.float32)
+    final_f32 = jnp.transpose(square)[:, :rows]
+    window = 16
+    row = lax.broadcasted_iota(jnp.int32, (window, shape_ref.shape[2]), 0)
+    wpart[pl.ds(0, LANES)] = jnp.zeros((LANES, shape_ref.shape[2]), jnp.float32)
     for e in range(elems):
-        part = jnp.dot(final_half, shape_ref[e], preferred_element_type=jnp.float32)
-        weighted = weighted + jnp.where((row >= RHS * e) & (row < RHS * e + RHS), part, 0.0)
-    wpart[pl.ds(0, LANES)] = -weighted
+        low = (RHS * e) // 8 * 8
+        part = jnp.dot(
+            final_f32[low:low + window].astype(jnp.bfloat16),
+            shape_ref[e],
+            preferred_element_type=jnp.float32,
+        )
+        mine = (row + low >= RHS * e) & (row + low < RHS * e + RHS)
+        wpart[pl.ds(low, window)] = wpart[pl.ds(low, window)] - jnp.where(mine, part, 0.0)
     chunk = wsum_ref.shape[0]
     owners = pl.cdiv(elems * RHS, chunk)
 

time: 72.3 us -> 72 us (level)
  no operation moved by 1% of the time
where the time goes in v11:
time: 72 us; the launch traced here: 71.7 us
  Pallas kernels  59.1 us (82%)
  local copies, waits for them, and re-layouts  6.97 us (10%)
  other arithmetic  4.88 us (7%)
  between operations  0.77 us (1%)
    pallas_call x1, Pallas kernels, sweeps(): pl.pallas_call(_sweeps_kernel, out_shape=(jax.ShapeDtypeStruct((rows, LAN...  45.6 us
    pallas_call x1, Pallas kernels, _exchange(): pl.pallas_call(kernel, out_shape=jax.ShapeDtypeStruct(out_shape, x.dtype)...  13.5 us
    unnamed x6, local copies, waits for them, and re-layouts  3.15 us
    scatter-add x1, other arithmetic, local(): partial_sums = jax.ops.segment_sum(values, node_slots, 3 * NODE_DEV).T  2.54 us

profile of v11, /device:TPU:7, one launch (start us, length us, event | category | flops | bytes accessed | tf_op | source)
XLA Modules:
  0.0 71.7 jit_solution(10587569483292152155)
XLA Ops:
  0.6 0.0 copy-start
  0.7 0.8 %dynamic-slice_subtract_fusion = s32[8,64]{1,0:T(8,128)S(1)} fusion(s32[24,64]{1,0:T(8,128)} %param.15, s32[]{:T(128)S(6)} %select_n.25, s32[]{:T(128)S(6)} %mul.35), kind=kLoop, calls=%fused_computation.11 | loop fusion | flops 512 | bytes 4104 | tf_op jit(solution)/shard_map/sub | solution.py:482
  1.5 0.1 reshape.94
  1.6 0.7 broadcast_subtract_fusion
  2.3 0.1 copy.22
  2.4 0.1 add.77
  2.5 0.1 copy.23
  2.6 0.7 %stack_broadcast_in_dim.2 = f32[1,24,3,80]{3,1,2,0:T(8,128)S(1)} broadcast(f32[24]{0:T(128)} %param.13), dimensions={1} | broadcast | bytes 23136 | tf_op jit(solution)/shard_map/stack;broadcast_in_dim | solution.py:402
  3.3 0.8 %maximum_bitcast_fusion = f32[3,80,24,3]{1,2,3,0:T(8,128)S(1)} fusion(f32[1,24,3,80]{3,1,2,0:T(8,128)S(1)} %stack_broadcast_in_dim.2, f32[1,24,3,80]{3,1,2,0:T(8,128)} %bitcast.30, f32[1,24,3,80]{3,1,2,0:T(8,128)} %bitcast.31), kind=kLoop, calls=%fused_computation.3 | loop fusion | flops 34560 | bytes 138240 | tf_op jit(solution)/shard_map/transpose | solution.py:407
  4.2 0.1 reshape.86
  4.2 0.1 copy.21
  4.4 0.0 copy-done
  4.4 0.0 copy-start.1
  4.4 1.2 %copy-done.1 = bf16[24,80,192]{2,1,0:T(8,128)(2,1)S(1)} copy-done((bf16[24,80,192]{2,1,0:T(8,128)(2,1)S(1)}, bf16[24,80,192]{2,1,0:T(8,128)(2,1)}, u32[]{:S(2)}) %copy-start.1) | copy-done | bytes 737304
  5.6 45.6 %shard_map.95 = (f32[80,128]{1,0:T(8,128)S(1)}, f32[24,192]{1,0:T(8,128)S(1)}) custom-call(f32[3,80,128]{2,1,0:T(8,128)S(1)} %pad.8.start_ref, s32[8,128]{1,0:T(8,128)S(1)} %pad.9.target_ref, bf16[24,7,80,320]{3,2,1,0:T(8,128)(2,1)} %jac_hbm.1, bf16[1920,320]{1,0:T(8,128)(2,1)S(1)} %bitcast.24, bf16[24,80,192]{2,1,0:T(8,128)(2,1)S(1)} %copy-done.1), custom_call_target="tpu_custom_call" | custom-call | tf_op jit(solution)/shard_map/pallas_call | solution.py:415
  51.2 0.1 copy.24
  51.3 0.6 copy.29
  51.9 0.7 %reshape.89 = f32[8,3,64,3]{3,2,1,0:T(8,128)S(1)} reshape(f32[24,192]{1,0:T(8,128)S(1)} %get-tuple-element.5) | data formatting | bytes 36864 | tf_op jit(solution)/shard_map/reshape | solution.py:476
  52.6 0.3 copy.25
  52.9 0.1 reshape.96
  53.0 0.1 copy.26
  53.2 2.5 %scatter_custom_fusion = f32[2304,9]{1,0:T(8,128)S(1)} fusion(s32[512]{0:T(512)S(1)} %reshape.94, f32[512,9]{1,0:T(8,128)S(1)} %copy.26, f32[]{:T(128)} %constant.15.clone.1), kind=kCustom, calls=%fused_computation.1 | custom fusion | flops 4608 | bytes 82948 | tf_op jit(solution)/shard_map/scatter-add | solution.py:483
  55.7 1.1 %copy.28 = f32[9,3,4,192]{3,0,2,1:T(8,128)} copy(f32[9,3,4,192]{0,3,2,1:T(8,128)S(1)} %bitcast.26) | data formatting | bytes 165888 | tf_op jit(solution)/shard_map/reshape | solution.py:485
  56.9 13.5 %shard_map.96 = f32[9,192]{1,0:T(8,128)} custom-call(f32[3,4,9,192]{3,2,1,0:T(8,128)} %bitcast.28), custom_call_target="tpu_custom_call" | custom-call | tf_op jit(solution)/shard_map/pallas_call | solution.py:158
  70.4 1.3 %copy.33 = f32[9,192]{1,0:T(8,128)} copy(f32[9,192]{1,0:T(8,128)} %shard_map.96) | data formatting | bytes 13824
  (10 shorter events, 0.2 us)
Async XLA Ops:
  0.6 3.7 %copy-start = (bf16[24,80,320]{2,1,0:T(8,128)(2,1)S(1)}, bf16[24,80,320]{2,1,0:T(8,128)(2,1)}, u32[]{:S(2)}) copy-start(bf16[24,80,320]{2,1,0:T(8,128)(2,1)} %param.11) | copy-start | bytes 3686404
  4.4 1.2 %copy-start.1 = (bf16[24,80,192]{2,1,0:T(8,128)(2,1)S(1)}, bf16[24,80,192]{2,1,0:T(8,128)(2,1)}, u32[]{:S(2)}) copy-start(bf16[24,80,192]{2,1,0:T(8,128)(2,1)} %shape_ref.1) | copy-start | bytes 2211844

commit v12 on v11

--- a/solution.py
+++ b/solution.py
@@ -196,8 +196,8 @@
 
 
 def _sweeps_kernel(
-    start_ref, target_ref, jac_hbm, inv_ref, shape_ref, out_ref, wsum_ref,
-    jac_v, select, send_a, halo, send_r, full_r, upd, jac_sem, hs_send, hs_recv, bk_send, bk_recv,
+    start_ref, target_ref, jac_hbm, inv_hbm, shape_hbm, out_ref, wsum_ref,
+    jac_v, inv_ref, shape_ref, select, send_a, halo, send_r, full_r, upd, jac_sem, hs_send, hs_recv, bk_send, bk_recv,
     fw_send, wpart, ws_send, ws_recv,
 ):
     d, b = lax.axis_index("dom"), lax.axis_index("blk")
@@ -210,8 +210,12 @@
         return (i >= 0) & (i < nd)
 
     partners = [(0, m) for m in range(1, nb)] + [(-1, 0), (1, 0)]
-    jac_copy = pltpu.make_async_copy(jac_hbm, jac_v, jac_sem)
+    jac_copy = pltpu.make_async_copy(jac_hbm, jac_v, jac_sem.at[0])
+    inv_copy = pltpu.make_async_copy(inv_hbm, inv_ref, jac_sem.at[1])
+    shape_copy = pltpu.make_async_copy(shape_hbm, shape_ref, jac_sem.at[2])
     jac_copy.start()
+    inv_copy.start()
+    shape_copy.start()
     _barrier(partners, in_range, d, b, nb)
     lane = lax.broadcasted_iota(jnp.int32, (rows, LANES), 1)
     cand_row = lax.broadcasted_iota(jnp.int32, (3 * LANES, LANES), 0)
@@ -329,6 +333,8 @@
                 device_id=(d, src_b),
                 device_id_type=MESH,
             ).wait_recv()
+        if sweep == 0:
+            inv_copy.wait()
         upd[...] = jnp.dot(
             inv_ref[...], full_r[sweep], preferred_element_type=jnp.float32
         ).reshape(upd.shape)
@@ -344,6 +350,7 @@
     window = 16
     row = lax.broadcasted_iota(jnp.int32, (window, shape_ref.shape[2]), 0)
     wpart[pl.ds(0, LANES)] = jnp.zeros((LANES, shape_ref.shape[2]), jnp.float32)
+    shape_copy.wait()
     for e in range(elems):
         low = (RHS * e) // 8 * 8
         part = jnp.dot(
@@ -411,6 +418,7 @@
     target = jnp.transpose(lanes, (1, 0, 2)).reshape(faces, elems * rhs)
     target = jnp.pad(target, ((0, 8 - faces), (0, LANES - elems * rhs)), constant_values=-1)
     vmem = pl.BlockSpec(memory_space=pltpu.VMEM)
+    hbm = pl.BlockSpec(memory_space=pl.ANY)
     chunk = 8 * rhs
     out, wsum = pl.pallas_call(
         _sweeps_kernel,
@@ -418,17 +426,19 @@
             jax.ShapeDtypeStruct((rows, LANES), jnp.float32),
             jax.ShapeDtypeStruct((chunk, shape_partials.shape[2]), jnp.float32),
         ),
-        in_specs=[vmem, vmem, pl.BlockSpec(memory_space=pl.ANY), vmem, vmem],
+        in_specs=[vmem, vmem, hbm, hbm, hbm],
         out_specs=(vmem, vmem),
         scratch_shapes=[
             pltpu.VMEM((elems, faces, rows, cols), jnp.bfloat16),
+            pltpu.VMEM((elems * rows, cols), jnp.bfloat16),
+            pltpu.VMEM(shape_partials.shape, shape_partials.dtype),
             pltpu.VMEM((faces, 3 * LANES, LANES), jnp.bfloat16),
             pltpu.VMEM((SWEEPS, rows, LANES), jnp.bfloat16),
             pltpu.VMEM((SWEEPS, 3, nb * rows, LANES), jnp.bfloat16),
             pltpu.VMEM((SWEEPS, rows, LANES), jnp.bfloat16),
             pltpu.VMEM((SWEEPS, nb * rows, LANES), jnp.bfloat16),
             pltpu.VMEM((elems, rows, LANES), jnp.float32),
-            pltpu.SemaphoreType.DMA(()),
+            pltpu.SemaphoreType.DMA((3,)),
             pltpu.SemaphoreType.DMA((SWEEPS, 3, nb)),
             pltpu.SemaphoreType.DMA((SWEEPS, 3, nb)),
             pltpu.SemaphoreType.DMA((SWEEPS, nb)),
@@ -439,7 +449,7 @@
             pltpu.SemaphoreType.DMA((nb,)),
         ],
         compiler_params=pltpu.CompilerParams(
-            collective_id=0, has_side_effects=True, vmem_limit_bytes=48 * 1024 * 1024
+            collective_id=0, has_side_effects=True, vmem_limit_bytes=67043328 - 640 * 1024
         ),
     )(
         stacked,

time: 72 us -> 75.2 us (1.044)
  Pallas kernels: 59.1 us -> 60.7 us
  local copies, waits for them, and re-layouts: 6.97 us -> 8.51 us
    pallas_call x1, Pallas kernels: 45.6 us -> 47.1 us  [sweeps(): pl.pallas_call(_sweeps_kernel, out_shape=(jax.ShapeDtypeStruct((rows, LAN...]
    unnamed x6 -> x2, local copies, waits for them, and re-layouts: 3.15 us -> 1.94 us
    slice x1, local copies, waits for them, and re-layouts: 0.07 us -> 0.85 us  [sweeps(): out[:, :elems * rhs].reshape(rows, elems, rhs)]
where the time goes in v12:
time: 75.2 us; the launch traced here: 74.7 us
  Pallas kernels  60.7 us (81%)
  local copies, waits for them, and re-layouts  8.51 us (11%)
  other arithmetic  4.78 us (6%)
    pallas_call x1, Pallas kernels, sweeps(): pl.pallas_call(_sweeps_kernel, out_shape=(jax.ShapeDtypeStruct((rows, LAN...  47.1 us
    pallas_call x1, Pallas kernels, _exchange(): pl.pallas_call(kernel, out_shape=jax.ShapeDtypeStruct(out_shape, x.dtype)...  13.5 us
    scatter-add x1, other arithmetic, local(): partial_sums = jax.ops.segment_sum(values, node_slots, 3 * NODE_DEV).T  2.54 us
    unnamed x2, local copies, waits for them, and re-layouts  1.94 us

profile of v12, /device:TPU:7, one launch (start us, length us, event | category | flops | bytes accessed | tf_op | source)
XLA Modules:
  0.0 74.7 jit_solution(8031480962185391296)
XLA Ops:
  0.6 0.7 dynamic-slice_subtract_fusion
  1.4 0.1 reshape.94
  1.4 0.7 broadcast_subtract_fusion
  2.2 0.1 copy.22
  2.2 0.1 add.77
  2.4 0.1 copy.23
  2.5 0.6 pad.9.target_ref
  3.1 0.7 stack_broadcast_in_dim.2
  3.8 0.8 %maximum_bitcast_fusion = f32[3,80,24,3]{1,2,3,0:T(8,128)S(1)} fusion(f32[1,24,3,80]{3,1,2,0:T(8,128)S(1)} %stack_broadcast_in_dim.2, f32[1,24,3,80]{3,1,2,0:T(8,128)} %bitcast.30, f32[1,24,3,80]{3,1,2,0:T(8,128)} %bitcast.31), kind=kLoop, calls=%fused_computation.3 | loop fusion | flops 34560 | bytes 138240 | tf_op jit(solution)/shard_map/transpose | solution.py:414
  4.7 0.1 reshape.86
  4.7 0.1 copy.21
  4.8 0.7 pad.8.start_ref
  5.5 47.1 %shard_map.95 = (f32[80,128]{1,0:T(8,128)}, f32[24,192]{1,0:T(8,128)}) custom-call(f32[3,80,128]{2,1,0:T(8,128)} %pad.8.start_ref, s32[8,128]{1,0:T(8,128)} %pad.9.target_ref, bf16[24,7,80,320]{3,2,1,0:T(8,128)(2,1)} %jac_hbm.1, bf16[1920,320]{1,0:T(8,128)(2,1)} %bitcast.26, bf16[24,80,192]{2,1,0:T(8,128)(2,1)} %shape_hbm.1), custom_call_target="tpu_custom_call" | custom-call | tf_op jit(solution)/shard_map/pallas_call | solution.py:423
  52.6 0.9 %copy.24 = f32[80,72]{0,1:T(8,128)S(1)} copy(f32[80,72]{1,0:T(8,128)} %bitcast.29) | data formatting | bytes 46080 | tf_op jit(solution)/shard_map/slice | solution.py:461
  53.5 0.6 copy.29
  54.1 1.5 %reshape.89 = f32[8,3,64,3]{3,2,1,0:T(8,128)S(1)} reshape(f32[24,192]{1,0:T(8,128)} %get-tuple-element.5) | data formatting | bytes 36864 | tf_op jit(solution)/shard_map/reshape | solution.py:486
  55.6 0.3 copy.25
  55.9 0.1 reshape.96
  56.0 0.1 copy.26
  56.1 2.5 %scatter_custom_fusion = f32[2304,9]{1,0:T(8,128)S(1)} fusion(s32[512]{0:T(512)S(1)} %reshape.94, f32[512,9]{1,0:T(8,128)S(1)} %copy.26, f32[]{:T(128)} %constant.15.clone.1), kind=kCustom, calls=%fused_computation.1 | custom fusion | flops 4608 | bytes 82948 | tf_op jit(solution)/shard_map/scatter-add | solution.py:493
  58.7 1.1 %copy.28 = f32[9,3,4,192]{3,0,2,1:T(8,128)} copy(f32[9,3,4,192]{0,3,2,1:T(8,128)S(1)} %bitcast.24) | data formatting | bytes 165888 | tf_op jit(solution)/shard_map/reshape | solution.py:495
  59.8 13.5 %shard_map.96 = f32[9,192]{1,0:T(8,128)} custom-call(f32[3,4,9,192]{3,2,1,0:T(8,128)} %bitcast.27), custom_call_target="tpu_custom_call" | custom-call | tf_op jit(solution)/shard_map/pallas_call | solution.py:158
  73.4 1.3 %copy.33 = f32[9,192]{1,0:T(8,128)} copy(f32[9,192]{1,0:T(8,128)} %shard_map.96) | data formatting | bytes 13824
  (8 shorter events, 0.1 us)
